TPU v7x, 128 devices: a whole 4x4x4 slice. The times are simulated.
128 devices in a mesh: dist: 16 (over x, z_hi, core), mem: 8 (over z_lo, y).
Axes of the slice: x: 4, y: 4, z: 4 (z_hi: 2, z_lo: 2; z = z_hi * 2 + z_lo), core: 2. Of those that a mesh axis runs over, the one named last changes fastest.
Arguments:
- anomalies: bfloat16 [128, 2048, 1024], P('dist', None, 'mem'), may hold values from -6 to 6
- innovations: bfloat16 [128, 256, 1024], P('dist', None, 'mem'), may hold values from -6 to 6
- obs_var: bfloat16 [128, 256], P('dist'), may hold values from 0.25 to 2
- node_pos: bfloat16 [2, 128, 2048], P(None, 'dist'), may hold values from 0 to 1
- obs_node: int32 [128, 256], P('dist'), may hold values from 0 to 2047
- obs_count: int32 [128], P('dist'), may hold values from 64 to 256, as said below
- in_radius: int32 [128, 7], P('dist'), may hold values from 0 to 1, as said below
Outputs:
- increment: float32 [128, 2048, 1024], P('dist', 'mem')
Inputs may be any that keep to these rules, and one draw needn't show every extreme that they name: `obs_count`: every district has at least 64 observations in use, and some district has all 256. `in_radius`: slot 3 (the district itself) is always 1; the ones of a district form a band of slots around it; slots naming a district outside 0 to 127 are 0; some district is paired with all districts up to 3 away.
All inputs are finite; a program needn't handle non-finite values.
Results may differ from a plain program's by a relative error of at most 0.0029.
Values may be sent and summed in bfloat16 or wider, within the bound.
A program may use at most 192 MiB of HBM per device.

v0:
```python
import functools
import jax
import jax.numpy as jnp
from jax import lax
from jax.experimental import pallas as pl
from jax.experimental.pallas import tpu as pltpu
from jax.sharding import PartitionSpec as P

MESH = pl.DeviceIdType.MESH
ANY = pl.BlockSpec(memory_space=pl.ANY)
VMEM = pl.BlockSpec(memory_space=pltpu.VMEM)
SMEM = pl.BlockSpec(memory_space=pltpu.SMEM)
DMA = pltpu.SemaphoreType.DMA
RADIUS = 3
REACH = 2.5


def prep_kernel(count_ref, anom_ref, innov_ref, node_ref, pos_ref, var_ref, src_ref, meta_ref, cols):
    d = pl.program_id(0)

    @pl.when(d == 0)
    def _():
        cols[...] = node_ref[...].T

    lane = lax.broadcasted_iota(jnp.int32, (256, 8), 1)
    node = jnp.sum(jnp.where(lane == d, cols[...], 0), axis=1, keepdims=True)
    slot = lax.broadcasted_iota(jnp.int32, (256, 1), 0)
    node = jnp.where(slot < count_ref[d], node, -1)
    hot = jnp.where(lax.broadcasted_iota(jnp.int32, (256, 2048), 1) == node, 1.0, 0.0).astype(jnp.bfloat16)
    src_ref[0, 0] = jnp.dot(hot, anom_ref[0], preferred_element_type=jnp.float32).astype(jnp.bfloat16)
    src_ref[1, 0] = innov_ref[0]
    spots = lax.dot_general(pos_ref[...], hot, (((1,), (1,)), ((), ())), preferred_element_type=jnp.float32)
    row16 = lax.broadcasted_iota(jnp.int32, (16, 256), 0)
    row8 = lax.broadcasted_iota(jnp.int32, (8, 256), 0)
    x = jnp.sum(jnp.where(row16 == d, spots, 0.0), axis=0, keepdims=True)
    yy = jnp.sum(jnp.where(row16 == d + 8, spots, 0.0), axis=0, keepdims=True)
    var = jnp.sum(jnp.where(row8 == d, var_ref[...].astype(jnp.float32), 0.0), axis=0, keepdims=True)
    meta_ref[0] = jnp.where(row8 == 0, x, jnp.where(row8 == 1, yy, jnp.where(row8 == 2, var, 0.0)))


def prep(anomalies, innovations, obs_var, node_pos, obs_node, obs_count):
    return pl.pallas_call(
        prep_kernel,
        grid=(8,),
        out_shape=(jax.ShapeDtypeStruct((2, 8, 256, 128), jnp.bfloat16), jax.ShapeDtypeStruct((8, 8, 256), jnp.float32)),
        in_specs=[
            SMEM,
            pl.BlockSpec((1, 2048, 128), lambda d: (d, 0, 0)),
            pl.BlockSpec((1, 256, 128), lambda d: (d, 0, 0)),
            VMEM,
            VMEM,
            VMEM,
        ],
        out_specs=(pl.BlockSpec((2, 1, 256, 128), lambda d: (0, d, 0, 0)), pl.BlockSpec((1, 8, 256), lambda d: (d, 0, 0))),
        scratch_shapes=[pltpu.VMEM((256, 8), jnp.int32)],
        compiler_params=pltpu.CompilerParams(vmem_limit_bytes=24 << 20),
    )(obs_count, anomalies, innovations, obs_node, node_pos.reshape(16, 2048), obs_var)


def exchange_kernel(anom, src, meta, xo, oi, mo, a_s, a_r, g_s, g_r, h_s, h_r, m_s, m_r, l_s):
    di, j = lax.axis_index("dist"), lax.axis_index("mem")
    core = lax.rem(di, 2)
    zl, y = j // 4, lax.rem(j, 4)

    def mem_of(z, row):
        return z * 4 + lax.rem(row + 8, 4)

    flip = mem_of(1 - zl, y)
    other = di + 1 - 2 * core
    remote = lax.rem(di + 15 + 2 * core, 16)
    barrier = pltpu.get_barrier_semaphore()
    for k in range(1, 8):
        pl.semaphore_signal(barrier, inc=1, device_id={"dist": di, "mem": lax.rem(j + k, 8)}, device_id_type=MESH)
    pl.semaphore_signal(barrier, inc=1, device_id={"dist": other, "mem": j}, device_id_type=MESH)
    pl.semaphore_signal(barrier, inc=1, device_id={"dist": remote, "mem": flip}, device_id_type=MESH)
    pl.semaphore_wait(barrier, 9)

    def remote_copy(source, target, send, recv, dist, mem):
        return pltpu.make_async_remote_copy(
            src_ref=source, dst_ref=target, send_sem=send, recv_sem=recv,
            device_id={"dist": dist, "mem": mem}, device_id_type=MESH)

    own_src = pltpu.make_async_copy(src, oi.at[:, pl.ds(3, 8), j], l_s.at[0])
    own_x = pltpu.make_async_copy(anom.at[:, pl.ds(pl.multiple_of(j * 256, 256), 256), :], xo.at[:, j], l_s.at[1])
    own_meta = pltpu.make_async_copy(meta, mo.at[pl.ds(3, 8)], l_s.at[2])
    own_src.start()
    own_x.start()
    own_meta.start()
    near_first = core == 1
    to_prev = remote_copy(
        meta.at[pl.ds(0, 3)], mo.at[pl.ds(11, 3)], m_s.at[0], m_r.at[0],
        jnp.where(near_first, other, remote), jnp.where(near_first, j, flip))
    to_next = remote_copy(
        meta.at[pl.ds(5, 3)], mo.at[pl.ds(0, 3)], m_s.at[1], m_r.at[1],
        jnp.where(near_first, remote, other), jnp.where(near_first, flip, j))
    to_prev.start()
    to_next.start()

    def a_copy(k, d):
        target = mem_of(lax.rem(zl + k // 4, 2), y + k % 4)
        return remote_copy(
            anom.at[d, pl.ds(pl.multiple_of(target * 256, 256), 256), :], xo.at[d, j],
            a_s.at[k - 1, d], a_r.at[k - 1, d], di, target)

    def unit(u):
        q = lax.rem(u, 8)
        return u // 8, q, q + core * (7 - 2 * q), 1 - 2 * lax.rem(u, 2)

    def own(u, edge):
        kind, q, d, s = unit(u)
        target = (mem_of(zl, y + s), mem_of(zl, y - s), flip)[edge]
        return remote_copy(src.at[kind, d], oi.at[kind, 3 + d, j], g_s.at[edge, u], g_r.at[edge, u], di, target)

    def forward(u, edge):
        kind, q, d, s = unit(u)
        held, target = {
            3: (mem_of(zl, y - s), flip),
            4: (mem_of(zl, y + s), mem_of(zl, y - s)),
            5: (flip, mem_of(zl, y - s)),
            6: (mem_of(1 - zl, y - s), mem_of(zl, y + s)),
        }[edge]
        block = oi.at[kind, 3 + d, held]
        return remote_copy(block, block, g_s.at[edge, u], g_r.at[edge, u], di, target)

    def gathered(u, edge):
        kind, q, d, s = unit(u)
        block = oi.at[kind, 3 + d, {
            0: mem_of(zl, y - s),
            1: mem_of(zl, y + s),
            2: flip,
            3: mem_of(1 - zl, y - s),
            4: mem_of(zl, y + 2),
            5: mem_of(1 - zl, y + s),
            6: mem_of(1 - zl, y + 2),
        }[edge]]
        return remote_copy(block, block, g_s.at[edge, u], g_r.at[edge, u], di, flip)

    def halo(u):
        kind, q, d, s = unit(u)
        near = q >= 5
        slot = jnp.where(d >= 5, d - 5, 11 + d)
        index = jnp.where(near, q - 2, q)
        return remote_copy(
            oi.at[kind, 3 + d], oi.at[kind, slot], h_s.at[kind, index], h_r.at[kind, index],
            jnp.where(near, other, remote), jnp.where(near, j, flip))

    def halo_in(kind, index):
        slot = jnp.where(core == 0, jnp.where(index < 3, 2 - index, 16 - index), jnp.where(index < 3, 11 + index, index - 3))
        return remote_copy(oi.at[kind, slot], oi.at[kind, slot], h_s.at[kind, index], h_r.at[kind, index], other, j)

    own_src.wait()

    def step(t, carry):
        @pl.when(t < 16)
        def _():
            for edge in range(3):
                own(t, edge).start()

        @pl.when((t < 16) & (lax.rem(t, 2) == 0))
        def _():
            for k in (6, 2, 5, 7, 4, 1, 3):
                a_copy(k, t // 2).start()

        u = t - 1

        @pl.when((u >= 0) & (u < 16))
        def _():
            for edge in range(3):
                gathered(u, edge).wait_recv()
                forward(u, edge + 3).start()

        v = t - 2

        @pl.when((v >= 0) & (v < 16))
        def _():
            gathered(v, 3).wait_recv()
            forward(v, 6).start()

        w = t - 3

        @pl.when((w >= 0) & (w < 16))
        def _():
            for edge in (4, 5, 6):
                gathered(w, edge).wait_recv()
            q = lax.rem(w, 8)

            @pl.when((q < 3) | (q >= 5))
            def _():
                halo(w).start()

        return carry

    lax.fori_loop(0, 19, step, 0)

    def drain(u, carry):
        for edge in range(7):
            gathered(u, edge).wait_send()
        q = lax.rem(u, 8)

        @pl.when((q < 3) | (q >= 5))
        def _():
            halo(u).wait_send()
            halo_in(u // 8, jnp.where(q >= 5, q - 2, q)).wait_recv()

        return carry

    lax.fori_loop(0, 16, drain, 0)

    def a_drain(d, carry):
        for k in range(1, 8):
            a_copy(k, d).wait_send()
            source = mem_of(lax.rem(zl + k // 4, 2), y + 4 - k % 4)
            block = xo.at[d, source]
            remote_copy(block, block, a_s.at[k - 1, d], a_r.at[k - 1, d], di, flip).wait_recv()
        return carry

    lax.fori_loop(0, 8, a_drain, 0)
    own_x.wait()
    own_meta.wait()
    to_prev.wait()
    to_next.wait()


def exchange(anom, src, meta):
    return pl.pallas_call(
        exchange_kernel,
        out_shape=(
            jax.ShapeDtypeStruct((8, 8, 256, 128), jnp.bfloat16),
            jax.ShapeDtypeStruct((2, 14, 8, 256, 128), jnp.bfloat16),
            jax.ShapeDtypeStruct((14, 8, 256), jnp.float32),
        ),
        in_specs=[ANY, ANY, ANY],
        out_specs=(ANY, ANY, ANY),
        scratch_shapes=[
            DMA((7, 8)), DMA((7, 8)), DMA((7, 16)), DMA((7, 16)), DMA((2, 6)), DMA((2, 6)), DMA((2,)), DMA((2,)), DMA((3,))],
        compiler_params=pltpu.CompilerParams(collective_id=0, has_side_effects=True, vmem_limit_bytes=8 << 20),
    )(anom, src, meta)


def pair_gain(cov, node_xy, meta, inv, shift):
    dx = (meta[0:1] + shift) - node_xy[:, 0:1]
    dy = meta[1:2] - node_xy[:, 1:2]
    square = jnp.maximum((dx * dx + dy * dy) * (1.0 / (REACH * REACH)), 1e-30)
    root = lax.rsqrt(square)
    z = square * root
    inner = (((-0.25 * z + 0.5) * z + 0.625) * z - 5.0 / 3.0) * square + 1.0
    left = jnp.maximum(2.0 - z, 0.0)
    left = left * left
    outer = (left * left) * (z * (1.0 / 12.0) + (1.0 / 6.0) - root * (1.0 / 24.0))
    return (jnp.where(z < 1.0, inner, outer) * cov * inv).astype(jnp.bfloat16)


def analysis_kernel(flag_ref, x_ref, xy_ref, meta_ref, oi_hbm, out_ref, oi, inv, cov, gain, sem):
    d = pl.program_id(0)

    def fetch(kind, e):
        return pltpu.make_async_copy(oi_hbm.at[kind, e], oi.at[kind, e], sem.at[kind, e])

    @pl.when(d == 0)
    def _():
        for e in range(14):
            for kind in range(2):
                fetch(kind, e).start()

    def full(kind, e):
        return jnp.concatenate([oi[kind, e, j] for j in range(8)], axis=1)

    def arrive(e):
        fetch(0, e).wait()
        fetch(1, e).wait()
        obs = full(0, e)
        gram = lax.dot_general(obs, obs, (((1,), (1,)), ((), ())), preferred_element_type=jnp.float32)
        same = lax.broadcasted_iota(jnp.int32, (256, 256), 0) == lax.broadcasted_iota(jnp.int32, (256, 256), 1)
        total = jnp.sum(jnp.where(same, gram, 0.0), axis=0, keepdims=True)
        inv[pl.ds(e, 1)] = 1.0 / (total + 1023.0 * meta_ref[e, 2:3])

    @pl.when(d == 0)
    def _():
        def one(e, c):
            arrive(e)
            return c
        lax.fori_loop(0, 7, one, 0)

    @pl.when(d > 0)
    def _():
        arrive(d + 6)

    def pair(s):
        e = d + s
        x = jnp.concatenate([x_ref[0, j] for j in range(8)], axis=1)
        cov[...] = lax.dot_general(x, full(0, e), (((1,), (1,)), ((), ())), preferred_element_type=jnp.float32)
        meta, row = meta_ref[e], inv[pl.ds(e, 1)]
        shift = (s - RADIUS).astype(jnp.float32)

        def rows(i, c):
            r = pl.ds(pl.multiple_of(i * 32, 32), 32)
            gain[r] = pair_gain(cov[r], xy_ref[0, r], meta, row, shift)
            return c

        lax.fori_loop(0, 8, rows, 0)
        return jnp.dot(gain[...], full(1, e), preferred_element_type=jnp.float32)

    out_ref[0] = pair(jnp.int32(RADIUS))

    def slots(s, c):
        @pl.when((s != RADIUS) & (flag_ref[d, s] > 0))
        def _():
            out_ref[0] += pair(s)
        return c

    lax.fori_loop(0, 7, slots, 0)


def analysis(in_radius, xs, own_xy, meta, oi):
    return pl.pallas_call(
        analysis_kernel,
        grid=(8,),
        out_shape=jax.ShapeDtypeStruct((8, 256, 1024), jnp.float32),
        in_specs=[
            SMEM,
            pl.BlockSpec((1, 8, 256, 128), lambda d: (d, 0, 0, 0)),
            pl.BlockSpec((1, 256, 2), lambda d: (d, 0, 0)),
            VMEM,
            ANY,
        ],
        out_specs=pl.BlockSpec((1, 256, 1024), lambda d: (d, 0, 0)),
        scratch_shapes=[
            pltpu.VMEM((2, 14, 8, 256, 128), jnp.bfloat16),
            pltpu.VMEM((14, 256), jnp.float32),
            pltpu.VMEM((256, 256), jnp.float32),
            pltpu.VMEM((256, 256), jnp.bfloat16),
            DMA((2, 14)),
        ],
        compiler_params=pltpu.CompilerParams(vmem_limit_bytes=40 << 20),
    )(in_radius, xs, own_xy, meta, oi)


def on_device(anomalies, innovations, obs_var, node_pos, obs_node, obs_count, in_radius):
    src, meta = prep(anomalies, innovations, obs_var, node_pos, obs_node, obs_count)
    own_xy = lax.dynamic_slice_in_dim(node_pos, lax.axis_index("mem") * 256, 256, 2)
    own_xy = jnp.transpose(own_xy, (1, 2, 0)).astype(jnp.float32)
    xs, oi, meta = exchange(anomalies, src, meta)
    return analysis(in_radius, xs, own_xy, meta, oi)


def solution(mesh):
    return jax.shard_map(
        on_device,
        mesh=mesh,
        in_specs=(
            P("dist", None, "mem"),
            P("dist", None, "mem"),
            P("dist", None),
            P(None, "dist", None),
            P("dist", None),
            P("dist"),
            P("dist", None),
        ),
        out_specs=P("dist", "mem", None),
        check_vma=False,
    )
```

profile of v0, /device:TPU:67, one launch (start us, length us, event | category | flops | bytes accessed | tf_op | source)
XLA Modules:
  0.0 200.0 jit_solution(10089464654511920737)
XLA Ops:
  0.0 0.0 copy-start.6
  0.0 0.7 constant_dynamic-slice_fusion
  0.7 0.4 copy.9
  1.1 0.1 convert_bitcast_fusion.xy_ref
  1.2 0.0 copy-start
  1.2 2.2 %copy-done = bf16[8,2048,128]{2,1,0:T(8,128)(2,1)S(1)} copy-done((bf16[8,2048,128]{2,1,0:T(8,128)(2,1)S(1)}, bf16[8,2048,128]{2,1,0:T(8,128)(2,1)}, u32[]{:S(2)}) %copy-start) | copy-done | bytes 4194328
  3.4 0.0 copy-start.3
  3.4 1.0 copy-done.3
  4.4 0.0 copy-start.4
  4.4 0.8 copy-done.4
  5.2 0.0 copy-start.5
  5.2 0.7 copy-done.5
  5.9 0.0 copy-start.7
  5.9 0.7 copy-done.7
  6.6 0.0 copy-start.8
  6.6 0.7 copy-done.8
  7.3 7.0 %shard_map.73 = (bf16[2,8,256,128]{3,2,1,0:T(8,128)(2,1)S(1)}, f32[8,8,256]{2,1,0:T(8,128)S(1)}) custom-call(s32[8]{0:T(128)S(1)} %copy-done.8, bf16[8,2048,128]{2,1,0:T(8,128)(2,1)S(1)} %copy-done, bf16[8,256,128]{2,1,0:T(8,128)(2,1)S(1)} %copy-done.3, s32[8,256]{1,0:T(8,128)S(1)} %copy-done.5, bf16[16,2048]{1,0:T(8,128)(2,1)S(1)} %bitcast.3, ...), custom_call_target="tpu_custom_call" | custom-call | tf_op jit(solution)/shard_map/pallas_call | solution.py:42
  14.3 0.0 copy-start.1
  14.3 2.2 %copy-done.1 = bf16[8,2048,128]{2,1,0:T(8,128)(2,1)S(1)} copy-done((bf16[8,2048,128]{2,1,0:T(8,128)(2,1)S(1)}, bf16[8,2048,128]{2,1,0:T(8,128)(2,1)}, u32[]{:S(2)}) %copy-start.1) | copy-done | bytes 4194328
  16.5 114.5 %shard_map.74 = (bf16[8,8,256,128]{3,2,1,0:T(8,128)(2,1)S(1)}, bf16[2,14,8,256,128]{4,3,2,1,0:T(8,128)(2,1)S(1)}, f32[14,8,256]{2,1,0:T(8,128)S(1)}) custom-call(bf16[8,2048,128]{2,1,0:T(8,128)(2,1)S(1)} %copy-done.1, bf16[2,8,256,128]{3,2,1,0:T(8,128)(2,1)S(1)} %get-tuple-element.10.src, f32[8,8,256]{2,1,0:T(8,128)S(1)} %get-tuple-element.11.meta), custom_call_target="tpu_custom_call" | custom-call | tf_op jit(solution)/shard_map/pallas_call | solution.py:225
  131.0 0.0 copy-start.2
  131.0 5.2 %copy-done.2 = bf16[2,14,8,256,128]{4,3,2,1,0:T(8,128)(2,1)} copy-done((bf16[2,14,8,256,128]{4,3,2,1,0:T(8,128)(2,1)}, bf16[2,14,8,256,128]{4,3,2,1,0:T(8,128)(2,1)S(1)}, u32[]{:S(2)}) %copy-start.2) | copy-done | bytes 14680088
  136.2 0.0 copy-done.6
  136.2 63.8 %shard_map.75 = f32[8,256,1024]{2,1,0:T(8,128)} custom-call(s32[8,7]{1,0:T(8,128)S(1)} %copy-done.6, bf16[8,8,256,128]{3,2,1,0:T(8,128)(2,1)S(1)} %get-tuple-element.12.x_ref, f32[8,256,2]{2,1,0:T(8,128)S(1)} %convert_bitcast_fusion.xy_ref, f32[14,8,256]{2,1,0:T(8,128)S(1)} %get-tuple-element.13.meta_ref, bf16[2,14,8,256,128]{4,3,2,1,0:T(8,128)(2,1)} %copy-done.2), custom_call_target="tpu_custom_call" | custom-call | tf_op jit(solution)/shard_map/pallas_call | solution.py:315
Async XLA Ops:
  0.0 136.2 %copy-start.6 = (s32[8,7]{1,0:T(8,128)S(1)}, s32[8,7]{1,0:T(8,128)}, u32[]{:S(2)}) copy-start(s32[8,7]{1,0:T(8,128)} %flag_ref.1) | copy-start | bytes 676
  1.2 2.2 %copy-start = (bf16[8,2048,128]{2,1,0:T(8,128)(2,1)S(1)}, bf16[8,2048,128]{2,1,0:T(8,128)(2,1)}, u32[]{:S(2)}) copy-start(bf16[8,2048,128]{2,1,0:T(8,128)(2,1)} %anom.1) | copy-start | bytes 12582916
  3.4 1.0 copy-start.3
  4.4 0.8 copy-start.4
  5.2 0.7 copy-start.5
  5.9 0.7 copy-start.7
  6.6 0.7 copy-start.8
  14.3 2.2 %copy-start.1 = (bf16[8,2048,128]{2,1,0:T(8,128)(2,1)S(1)}, bf16[8,2048,128]{2,1,0:T(8,128)(2,1)}, u32[]{:S(2)}) copy-start(bf16[8,2048,128]{2,1,0:T(8,128)(2,1)} %anom.1) | copy-start | bytes 12582916
  131.0 5.2 %copy-start.2 = (bf16[2,14,8,256,128]{4,3,2,1,0:T(8,128)(2,1)}, bf16[2,14,8,256,128]{4,3,2,1,0:T(8,128)(2,1)S(1)}, u32[]{:S(2)}) copy-start(bf16[2,14,8,256,128]{4,3,2,1,0:T(8,128)(2,1)S(1)} %get-tuple-element.14.oi_hbm) | copy-start | bytes 44040196
where the time goes:
time: 200 us
  Pallas kernels  185 us (92%)
  local copies, waits for them, and re-layouts  14.6 us (7%)
    pallas_call x1, Pallas kernels, exchange(): pl.pallas_call(exchange_kernel, out_shape=(jax.ShapeDtypeStruct((8, 8, 25...  114 us
    pallas_call x1, Pallas kernels, analysis(): pl.pallas_call(analysis_kernel, grid=(8,), out_shape=jax.ShapeDtypeStruct...  63.8 us
    unnamed x19, local copies, waits for them, and re-layouts  13.8 us
    pallas_call x1, Pallas kernels, prep(): pl.pallas_call(prep_kernel, grid=(8,), out_shape=(jax.ShapeDtypeStruct((2...  7 us

commit v1 on v0

v1 whole, which is shorter than its diff:
```python
import jax
import jax.numpy as jnp
from jax import lax
from jax.experimental import pallas as pl
from jax.experimental.pallas import tpu as pltpu
from jax.sharding import PartitionSpec as P

MESH = pl.DeviceIdType.MESH
HBM = pl.BlockSpec(memory_space=pltpu.HBM)
VMEM = pl.BlockSpec(memory_space=pltpu.VMEM)
SMEM = pl.BlockSpec(memory_space=pltpu.SMEM)
DMA = pltpu.SemaphoreType.DMA
RADIUS = 3
REACH = 2.5
UNITS = 16
LAG = 2
FAR_FIRST = (6, 2, 5, 7, 4, 1, 3)


def exchange_kernel(
    anom, innov, node_h, count_h, pos_h, var_h, xo, oi, mo, xy_o,
    held, seen, meta, xy, node, count, pos, var, cols,
    a_s, a_r, g_s, g_r, h_s, h_r, m_s, m_r, l_s, p_s, w_s,
):
    di, j = lax.axis_index("dist"), lax.axis_index("mem")
    core = lax.rem(di, 2)
    zl, y = j // 4, lax.rem(j, 4)

    def mem_of(z, row):
        return z * 4 + lax.rem(row + 8, 4)

    def district(q):
        return q + core * (7 - 2 * q)

    small = [
        pltpu.make_async_copy(node_h, node, l_s.at[0]),
        pltpu.make_async_copy(count_h, count, l_s.at[1]),
        pltpu.make_async_copy(pos_h, pos, l_s.at[2]),
        pltpu.make_async_copy(var_h, var, l_s.at[3]),
    ]
    for copy in small:
        copy.start()

    def load(q):
        return pltpu.make_async_copy(anom.at[district(q)], held.at[lax.rem(q, 2)], p_s.at[lax.rem(q, 2)])

    load(0).start()
    load(1).start()
    own_x = pltpu.make_async_copy(anom.at[:, pl.ds(pl.multiple_of(j * 256, 256), 256), :], xo.at[:, j], l_s.at[4])
    own_innov = pltpu.make_async_copy(innov, oi.at[1, pl.ds(3, 8), j], l_s.at[5])
    own_x.start()
    own_innov.start()

    flip = mem_of(1 - zl, y)
    other = di + 1 - 2 * core
    remote = lax.rem(di + 15 + 2 * core, 16)
    barrier = pltpu.get_barrier_semaphore()
    for k in range(1, 8):
        pl.semaphore_signal(barrier, inc=1, device_id={"dist": di, "mem": lax.rem(j + k, 8)}, device_id_type=MESH)
    pl.semaphore_signal(barrier, inc=1, device_id={"dist": other, "mem": j}, device_id_type=MESH)
    pl.semaphore_signal(barrier, inc=1, device_id={"dist": remote, "mem": flip}, device_id_type=MESH)
    pl.semaphore_wait(barrier, 9)

    def remote_copy(source, target, send, recv, dist, mem):
        return pltpu.make_async_remote_copy(
            src_ref=source, dst_ref=target, send_sem=send, recv_sem=recv,
            device_id={"dist": dist, "mem": mem}, device_id_type=MESH)

    def spread_nodes(k, q):
        d = district(q)
        target = mem_of(lax.rem(zl + k // 4, 2), y + k % 4)
        return remote_copy(
            anom.at[d, pl.ds(pl.multiple_of(target * 256, 256), 256), :], xo.at[d, j],
            a_s.at[k - 1, q], a_r.at[k - 1, q], di, target)

    def unit(u):
        early = u < 6
        kind = jnp.where(early, u // 3, (u - 6) // 5)
        q = jnp.where(early, lax.rem(u, 3), 3 + lax.rem(u + 4, 5))
        return kind, q, district(q), 1 - 2 * lax.rem(u, 2), lax.rem(u, 3) == 2

    def edge_copy(u, edge, source, block, mem):
        return remote_copy(source, block, g_s.at[edge, u], g_r.at[edge, u], di, mem)

    def forward(u, edge):
        kind, q, d, s, three = unit(u)
        here, there = zl, 1 - zl
        from_, to = {
            3: (mem_of(here, y - s), flip),
            4: (mem_of(here, y + s), jnp.where(three, flip, mem_of(here, y - s))),
            5: (jnp.where(three, mem_of(here, y - s), flip), jnp.where(three, mem_of(here, y + s), mem_of(here, y - s))),
            6: (jnp.where(three, mem_of(there, y + s), mem_of(there, y - s)),
                jnp.where(three, mem_of(here, y - s), mem_of(here, y + s))),
        }[edge]
        block = oi.at[kind, 3 + d, from_]
        return edge_copy(u, edge, block, block, to)

    def gathered(u, edge):
        kind, q, d, s, three = unit(u)
        here, there = zl, 1 - zl
        from_ = (
            mem_of(here, y - s),
            mem_of(here, y + s),
            flip,
            mem_of(there, y - s),
            jnp.where(three, mem_of(there, y + s), mem_of(here, y + 2)),
            jnp.where(three, mem_of(here, y + 2), mem_of(there, y + s)),
            mem_of(there, y + 2),
        )[edge]
        block = oi.at[kind, 3 + d, from_]
        return edge_copy(u, edge, block, block, flip)

    def halo(u):
        kind, q, d, s, three = unit(u)
        near = q >= 5
        slot = jnp.where(d >= 5, d - 5, 11 + d)
        index = jnp.where(near, q - 2, q)
        return remote_copy(
            oi.at[kind, 3 + d], oi.at[kind, slot], h_s.at[kind, index], h_r.at[kind, index],
            jnp.where(near, other, remote), jnp.where(near, j, flip))

    def halo_in(kind, index):
        slot = jnp.where(core == 0, jnp.where(index < 3, 2 - index, 16 - index), jnp.where(index < 3, 11 + index, index - 3))
        return remote_copy(oi.at[kind, slot], oi.at[kind, slot], h_s.at[kind, index], h_r.at[kind, index], other, j)

    def has_halo(u):
        q = unit(u)[1]
        return (q < 3) | (q >= 5)

    def own_seen(d):
        return pltpu.make_async_copy(seen.at[d], oi.at[0, 3 + d, j], w_s.at[d])

    for k in FAR_FIRST:
        spread_nodes(k, 0).start()
    for copy in small:
        copy.wait()
    slot8 = lax.broadcasted_iota(jnp.int32, (256, 8), 0)
    cols[...] = jnp.where(slot8 < count[...], node[...].T, -1)
    xy[...] = pos[:, pl.ds(pl.multiple_of(j * 256, 256), 256)].astype(jnp.float32).T

    def observe(q):
        d = district(q)
        load(q).wait()
        lane = lax.broadcasted_iota(jnp.int32, (256, 8), 1)
        which = jnp.sum(jnp.where(lane == d, cols[...], 0), axis=1, keepdims=True)
        hot = jnp.where(lax.broadcasted_iota(jnp.int32, (256, 2048), 1) == which, 1.0, 0.0).astype(jnp.bfloat16)
        rows = jnp.dot(hot, held[lax.rem(q, 2)], preferred_element_type=jnp.float32)
        seen[d] = rows.astype(jnp.bfloat16)
        spots = lax.dot_general(pos[...], hot, (((1,), (1,)), ((), ())), preferred_element_type=jnp.float32)
        row16 = lax.broadcasted_iota(jnp.int32, (16, 256), 0)
        row8 = lax.broadcasted_iota(jnp.int32, (8, 256), 0)
        sx = jnp.sum(jnp.where(row16 == d, spots, 0.0), axis=0, keepdims=True)
        sy = jnp.sum(jnp.where(row16 == d + 8, spots, 0.0), axis=0, keepdims=True)
        sv = jnp.sum(jnp.where(row8 == d, var[...].astype(jnp.float32), 0.0), axis=0, keepdims=True)
        meta[d] = jnp.where(row8 == 0, sx, jnp.where(row8 == 1, sy, jnp.where(row8 == 2, sv, 0.0)))

        @pl.when(q < 6)
        def _():
            load(q + 2).start()

        own_seen(d).start()

    near_first = core == 1
    to_prev = remote_copy(
        meta.at[pl.ds(0, 3)], mo.at[pl.ds(11, 3)], m_s.at[0], m_r.at[0],
        jnp.where(near_first, other, remote), jnp.where(near_first, j, flip))
    to_next = remote_copy(
        meta.at[pl.ds(5, 3)], mo.at[pl.ds(0, 3)], m_s.at[1], m_r.at[1],
        jnp.where(near_first, remote, other), jnp.where(near_first, flip, j))
    own_meta = pltpu.make_async_copy(meta, mo.at[pl.ds(3, 8)], l_s.at[0])
    own_xy = pltpu.make_async_copy(xy, xy_o, l_s.at[1])
    own_xy.start()

    def step(t, carry):
        @pl.when(t < UNITS)
        def _():
            kind, q, d, s, three = unit(t)
            targets = (mem_of(zl, y + s), mem_of(zl, y - s), flip)

            @pl.when(kind == 0)
            def _():
                observe(q)
                for edge in range(3):
                    edge_copy(t, edge, seen.at[d], oi.at[0, 3 + d, j], targets[edge]).start()

            @pl.when(kind == 1)
            def _():
                for edge in range(3):
                    edge_copy(t, edge, innov.at[d], oi.at[1, 3 + d, j], targets[edge]).start()

        @pl.when((t >= 2) & (t < UNITS) & (lax.rem(t, 2) == 0))
        def _():
            for k in FAR_FIRST:
                spread_nodes(k, t // 2).start()

        @pl.when(t == 11)
        def _():
            to_prev.start()
            to_next.start()
            own_meta.start()

        u = t - LAG

        @pl.when((u >= 0) & (u < UNITS))
        def _():
            for edge in range(3):
                gathered(u, edge).wait_recv()
                forward(u, edge + 3).start()

        v = t - 2 * LAG

        @pl.when((v >= 0) & (v < UNITS))
        def _():
            gathered_last(v, True)
            forward(v, 6).start()

        w = t - 3 * LAG

        @pl.when((w >= 0) & (w < UNITS))
        def _():
            gathered_last(w, False)
            gathered(w, 5).wait_recv()
            gathered(w, 6).wait_recv()
            kind, q, d, s, three = unit(w)

            @pl.when(kind == 0)
            def _():
                own_seen(d).wait()

            @pl.when(w == 3)
            def _():
                own_innov.wait()

            @pl.when(has_halo(w))
            def _():
                halo(w).start()

        return carry

    def gathered_last(u, first):
        three = unit(u)[4]
        take4 = three if first else jnp.logical_not(three)

        @pl.when(take4)
        def _():
            gathered(u, 4).wait_recv()

        @pl.when(jnp.logical_not(take4))
        def _():
            gathered(u, 3).wait_recv()

    lax.fori_loop(0, UNITS + 3 * LAG, step, 0)

    def drain(u, carry):
        for edge in range(7):
            gathered(u, edge).wait_send()

        @pl.when(has_halo(u))
        def _():
            kind, q, d, s, three = unit(u)
            halo(u).wait_send()
            halo_in(kind, jnp.where(q >= 5, q - 2, q)).wait_recv()

        return carry

    lax.fori_loop(0, UNITS, drain, 0)

    def drain_nodes(q, carry):
        for k in range(1, 8):
            spread_nodes(k, q).wait_send()
            source = mem_of(lax.rem(zl + k // 4, 2), y + 4 - k % 4)
            block = xo.at[district(q), source]
            remote_copy(block, block, a_s.at[k - 1, q], a_r.at[k - 1, q], di, flip).wait_recv()
        return carry

    lax.fori_loop(0, 8, drain_nodes, 0)
    own_x.wait()
    own_meta.wait()
    own_xy.wait()
    to_prev.wait()
    to_next.wait()


def exchange(anomalies, innovations, obs_var, node_pos, obs_node, obs_count):
    return pl.pallas_call(
        exchange_kernel,
        out_shape=(
            jax.ShapeDtypeStruct((8, 8, 256, 128), jnp.bfloat16),
            jax.ShapeDtypeStruct((2, 14, 8, 256, 128), jnp.bfloat16),
            jax.ShapeDtypeStruct((14, 8, 256), jnp.float32),
            jax.ShapeDtypeStruct((256, 16), jnp.float32),
        ),
        in_specs=[HBM] * 6,
        out_specs=(HBM,) * 4,
        scratch_shapes=[
            pltpu.VMEM((2, 2048, 128), jnp.bfloat16),
            pltpu.VMEM((8, 256, 128), jnp.bfloat16),
            pltpu.VMEM((8, 8, 256), jnp.float32),
            pltpu.VMEM((256, 16), jnp.float32),
            pltpu.VMEM((8, 256), jnp.int32),
            pltpu.VMEM((1, 8), jnp.int32),
            pltpu.VMEM((16, 2048), jnp.bfloat16),
            pltpu.VMEM((8, 256), jnp.bfloat16),
            pltpu.VMEM((256, 8), jnp.int32),
            DMA((7, 8)), DMA((7, 8)), DMA((7, UNITS)), DMA((7, UNITS)), DMA((2, 6)), DMA((2, 6)), DMA((2,)), DMA((2,)),
            DMA((6,)), DMA((2,)), DMA((8,)),
        ],
        compiler_params=pltpu.CompilerParams(collective_id=0, has_side_effects=True, vmem_limit_bytes=56 << 20),
    )(anomalies, innovations, obs_node, obs_count.reshape(1, 8), node_pos.reshape(16, 2048), obs_var)


def taper(node_x, node_y, meta, shift):
    dx = (meta[0:1] + shift) - node_x
    dy = meta[1:2] - node_y
    square = jnp.maximum((dx * dx + dy * dy) * (1.0 / (REACH * REACH)), 1e-30)
    root = lax.rsqrt(square)
    z = square * root
    inner = (((-0.25 * z + 0.5) * z + 0.625) * z - 5.0 / 3.0) * square + 1.0
    left = jnp.maximum(2.0 - z, 0.0)
    left = left * left
    outer = (left * left) * (z * (1.0 / 12.0) + (1.0 / 6.0) - root * (1.0 / 24.0))
    return jnp.where(z < 1.0, inner, outer)


def analysis_kernel(flag_ref, x_ref, xy_ref, meta_ref, oi_hbm, out_ref, oi, inv, cov, gain, sem):
    d = pl.program_id(0)

    def fetch(kind, e):
        return pltpu.make_async_copy(oi_hbm.at[kind, e], oi.at[kind, e], sem.at[kind, e])

    @pl.when(d == 0)
    def _():
        for e in range(14):
            for kind in range(2):
                fetch(kind, e).start()

    def full(kind, e):
        return jnp.concatenate([oi[kind, e, j] for j in range(8)], axis=1)

    def arrive(e):
        fetch(0, e).wait()
        fetch(1, e).wait()
        total = jnp.zeros((256, 128), jnp.float32)
        for j in range(8):
            part = oi[0, e, j].astype(jnp.float32)
            total = total + part * part
        total = jnp.sum(total.T, axis=0, keepdims=True)
        inv[pl.ds(e, 1)] = 1.0 / (total + 1023.0 * meta_ref[e, 2:3])

    @pl.when(d == 0)
    def _():
        def one(e, c):
            arrive(e)
            return c
        lax.fori_loop(0, 7, one, 0)

    @pl.when(d > 0)
    def _():
        arrive(d + 6)

    lane = lax.broadcasted_iota(jnp.int32, (256, 16), 1)
    node_x = jnp.sum(jnp.where(lane == d, xy_ref[...], 0.0), axis=1, keepdims=True)
    node_y = jnp.sum(jnp.where(lane == d + 8, xy_ref[...], 0.0), axis=1, keepdims=True)

    def pair(s):
        e = d + s
        x = jnp.concatenate([x_ref[0, j] for j in range(8)], axis=1)
        cov[...] = lax.dot_general(x, full(0, e), (((1,), (1,)), ((), ())), preferred_element_type=jnp.float32)
        meta, row = meta_ref[e], inv[pl.ds(e, 1)]
        shift = (s - RADIUS).astype(jnp.float32)
        for i in range(0, 256, 32):
            r = slice(i, i + 32)
            gain[r] = (taper(node_x[r], node_y[r], meta, shift) * cov[r] * row).astype(jnp.bfloat16)
        return jnp.dot(gain[...], full(1, e), preferred_element_type=jnp.float32)

    out_ref[0] = pair(jnp.int32(RADIUS))

    def slots(s, c):
        @pl.when((s != RADIUS) & (flag_ref[d, s] > 0))
        def _():
            out_ref[0] += pair(s)
        return c

    lax.fori_loop(0, 7, slots, 0)


def analysis(in_radius, xs, own_xy, meta, oi):
    return pl.pallas_call(
        analysis_kernel,
        grid=(8,),
        out_shape=jax.ShapeDtypeStruct((8, 256, 1024), jnp.float32),
        in_specs=[
            SMEM,
            pl.BlockSpec((1, 8, 256, 128), lambda d: (d, 0, 0, 0)),
            VMEM,
            VMEM,
            HBM,
        ],
        out_specs=pl.BlockSpec((1, 256, 1024), lambda d: (d, 0, 0)),
        scratch_shapes=[
            pltpu.VMEM((2, 14, 8, 256, 128), jnp.bfloat16),
            pltpu.VMEM((14, 256), jnp.float32),
            pltpu.VMEM((256, 256), jnp.float32),
            pltpu.VMEM((256, 256), jnp.bfloat16),
            DMA((2, 14)),
        ],
        compiler_params=pltpu.CompilerParams(vmem_limit_bytes=56 << 20),
    )(in_radius, xs, own_xy, meta, oi)


def on_device(anomalies, innovations, obs_var, node_pos, obs_node, obs_count, in_radius):
    xs, oi, meta, own_xy = exchange(anomalies, innovations, obs_var, node_pos, obs_node, obs_count)
    return analysis(in_radius, xs, own_xy, meta, oi)


def solution(mesh):
    return jax.shard_map(
        on_device,
        mesh=mesh,
        in_specs=(
            P("dist", None, "mem"),
            P("dist", None, "mem"),
            P("dist", None),
            P(None, "dist", None),
            P("dist", None),
            P("dist"),
            P("dist", None),
        ),
        out_specs=P("dist", "mem", None),
        check_vma=False,
    )
```

time: 200 us -> 149 us (0.74)
  the two profiles are of different devices: /device:TPU:67 before, /device:TPU:1 now
where the time goes in v1:
time: 149 us; the launch traced here: 147 us
  Pallas kernels  147 us (99%)
    pallas_call x1, Pallas kernels, exchange(): pl.pallas_call(exchange_kernel, out_shape=(jax.ShapeDtypeStruct((8, 8, 25...  114 us
    pallas_call x1, Pallas kernels, analysis(): pl.pallas_call(analysis_kernel, grid=(8,), out_shape=jax.ShapeDtypeStruct...  33.3 us

profile of v1, /device:TPU:1, one launch (start us, length us, event | category | flops | bytes accessed | tf_op | source)
XLA Modules:
  0.0 147.3 jit_solution(3764178711899246384)
XLA Ops:
  0.0 114.0 %shard_map.73 = (bf16[8,8,256,128]{3,2,1,0:T(8,128)(2,1)}, bf16[2,14,8,256,128]{4,3,2,1,0:T(8,128)(2,1)}, f32[14,8,256]{2,1,0:T(8,128)}, f32[256,16]{1,0:T(8,128)}) custom-call(bf16[8,2048,128]{2,1,0:T(8,128)(2,1)} %anom.1, bf16[8,256,128]{2,1,0:T(8,128)(2,1)} %innov.1, s32[8,256]{1,0:T(8,128)} %node_h.1, s32[1,8]{1,0:T(1,128)} %bitcast.3, ...), custom_call_target="tpu_custom_call" | custom-call | tf_op jit(solution)/shard_map/pallas_call | solution.py:285
  114.0 33.3 %shard_map.74 = f32[8,256,1024]{2,1,0:T(8,128)} custom-call(s32[8,7]{1,0:T(8,128)} %flag_ref.1, bf16[8,8,256,128]{3,2,1,0:T(8,128)(2,1)} %get-tuple-element.9.x_ref, f32[256,16]{1,0:T(8,128)} %get-tuple-element.10.xy_ref, f32[14,8,256]{2,1,0:T(8,128)} %get-tuple-element.11.meta_ref, bf16[2,14,8,256,128]{4,3,2,1,0:T(8,128)(2,1)} %get-tuple-element.12.oi_hbm), custom_call_target="tpu_custom_call" | custom-call | tf_op jit(solution)/shard_map/pallas_call | solution.py:388

commit v2 on v1

v2 whole, which is shorter than its diff:
```python
import jax
import jax.numpy as jnp
from jax import lax
from jax.experimental import pallas as pl
from jax.experimental.pallas import tpu as pltpu
from jax.sharding import PartitionSpec as P

MESH = pl.DeviceIdType.MESH
HBM = pl.BlockSpec(memory_space=pltpu.HBM)
VMEM = pl.BlockSpec(memory_space=pltpu.VMEM)
SMEM = pl.BlockSpec(memory_space=pltpu.SMEM)
DMA = pltpu.SemaphoreType.DMA
RADIUS = 3
REACH = 2.5
UNITS = 16
LAG = 2
FAR_FIRST = (6, 2, 5, 7, 4, 1, 3)
STEPS = 25
X_STEP = (4, 5, 7, 8, 10, 11, 13, 14)


def column(*parts):
    items = [(e + 3) * 8 + d for e, own in parts for d in own]
    return sum(item * 128 ** i for i, item in enumerate(items))


GAIN_FIRST = 9
GAIN_TABLE = (
    column((0, (0, 1, 2, 3))),
    column((1, (0, 1, 2, 3))),
    column((1, (4,)), (-1, (0, 1, 2))),
    column((2, (0, 1, 2, 3))),
    column((2, (4, 5)), (-2, (0, 1))),
    column((7, (4, 5, 6)), (8, (5,))),
    column((7, (7,)), (8, (6, 7)), (-3, (0,))),
    column((6, (3, 4, 5, 6))),
    column((6, (7,)), (9, (6, 7)), (5, (2,))),
    column((5, (3, 4, 5, 6))),
    column((5, (7,)), (10, (7,)), (4, (1, 2))),
    column((4, (3, 4, 5, 6))),
    column((4, (7,)), (3, (0, 1, 2))),
    column((3, (3, 4, 5, 6))),
)
INC_FIRST = 10
INC_TABLE = (
    column((0, (0, 1, 2, 3))),
    column((1, (0, 1, 2, 3))),
    column((1, (4,)), (2, (0, 1, 2))),
    0,
    column((2, (3, 4, 5)), (7, (4,))),
    column((7, (5, 6, 7)), (8, (5,))),
    column((8, (6, 7)), (6, (3, 4))),
    column((6, (5, 6, 7)), (9, (6,))),
    column((9, (7,)), (-1, (0, 1, 2))),
    column((5, (2, 3, 4, 5))),
    column((5, (6, 7)), (10, (7,)), (-2, (0,))),
    column((-2, (1,)), (4, (1, 2, 3))),
    column((4, (4, 5, 6, 7))),
    column((-3, (0,)), (3, (0, 1, 2))),
    column((3, (3, 4, 5, 6))),
)


def analysis_kernel(
    anom, innov, node_h, count_h, pos_h, var_h, flags, out, xo, oi,
    held, seen, meta, node, count, pos, var, cols, xs, obs, inn, gains, total, inv, spot,
    a_s, a_r, g_s, g_r, h_s, h_r, m_s, m_r, l_s, p_s, w_s, v_s, x_s, o_s,
):
    di, j = lax.axis_index("dist"), lax.axis_index("mem")
    core = lax.rem(di, 2)
    zl, y = j // 4, lax.rem(j, 4)

    def mem_of(z, row):
        return z * 4 + lax.rem(row + 8, 4)

    def district(q):
        return q + core * (7 - 2 * q)

    small = [
        pltpu.make_async_copy(node_h, node, l_s.at[0]),
        pltpu.make_async_copy(count_h, count, l_s.at[1]),
        pltpu.make_async_copy(pos_h, pos, l_s.at[2]),
        pltpu.make_async_copy(var_h, var, l_s.at[3]),
    ]
    for copy in small:
        copy.start()

    def turn(n):
        return jnp.where(n < 3, n, 10 - n)

    def load(n):
        return pltpu.make_async_copy(anom.at[district(turn(n))], held.at[lax.rem(n, 2)], p_s.at[lax.rem(n, 2)])

    load(0).start()
    load(1).start()
    own_x = pltpu.make_async_copy(anom.at[:, pl.ds(pl.multiple_of(j * 256, 256), 256), :], xo.at[:, j], l_s.at[4])
    own_innov = pltpu.make_async_copy(innov, oi.at[1, pl.ds(3, 8), j], l_s.at[5])
    own_x.start()
    own_innov.start()

    flip = mem_of(1 - zl, y)
    other = di + 1 - 2 * core
    remote = lax.rem(di + 15 + 2 * core, 16)
    barrier = pltpu.get_barrier_semaphore()
    for k in range(1, 8):
        pl.semaphore_signal(barrier, inc=1, device_id={"dist": di, "mem": lax.rem(j + k, 8)}, device_id_type=MESH)
    pl.semaphore_signal(barrier, inc=1, device_id={"dist": other, "mem": j}, device_id_type=MESH)
    pl.semaphore_signal(barrier, inc=1, device_id={"dist": remote, "mem": flip}, device_id_type=MESH)
    pl.semaphore_wait(barrier, 9)

    def remote_copy(source, target, send, recv, dist, mem):
        return pltpu.make_async_remote_copy(
            src_ref=source, dst_ref=target, send_sem=send, recv_sem=recv,
            device_id={"dist": dist, "mem": mem}, device_id_type=MESH)

    def spread_nodes(k, q):
        d = district(q)
        target = mem_of(lax.rem(zl + k // 4, 2), y + k % 4)
        return remote_copy(
            anom.at[d, pl.ds(pl.multiple_of(target * 256, 256), 256), :], xo.at[d, j],
            a_s.at[k - 1, q], a_r.at[k - 1, q], di, target)

    def unit(u):
        early = u < 6
        kind = jnp.where(early, u // 3, lax.rem(u, 2))
        q = jnp.where(early, lax.rem(u, 3), 10 - u // 2)
        return kind, q, district(q), 1 - 2 * lax.rem(u, 2), lax.rem(u, 3) == 2

    def edge_copy(u, edge, source, block, mem):
        return remote_copy(source, block, g_s.at[edge, u], g_r.at[edge, u], di, mem)

    def forward(u, edge):
        kind, q, d, s, three = unit(u)
        here, there = zl, 1 - zl
        from_, to = {
            3: (mem_of(here, y - s), flip),
            4: (mem_of(here, y + s), jnp.where(three, flip, mem_of(here, y - s))),
            5: (jnp.where(three, mem_of(here, y - s), flip), jnp.where(three, mem_of(here, y + s), mem_of(here, y - s))),
            6: (jnp.where(three, mem_of(there, y + s), mem_of(there, y - s)),
                jnp.where(three, mem_of(here, y - s), mem_of(here, y + s))),
        }[edge]
        block = oi.at[kind, 3 + d, from_]
        return edge_copy(u, edge, block, block, to)

    def gathered(u, edge):
        kind, q, d, s, three = unit(u)
        here, there = zl, 1 - zl
        from_ = (
            mem_of(here, y - s),
            mem_of(here, y + s),
            flip,
            mem_of(there, y - s),
            jnp.where(three, mem_of(there, y + s), mem_of(here, y + 2)),
            jnp.where(three, mem_of(here, y + 2), mem_of(there, y + s)),
            mem_of(there, y + 2),
        )[edge]
        block = oi.at[kind, 3 + d, from_]
        return edge_copy(u, edge, block, block, flip)

    def halo(u):
        kind, q, d, s, three = unit(u)
        near = q >= 5
        slot = jnp.where(d >= 5, d - 5, 11 + d)
        index = jnp.where(near, q - 2, q)
        return remote_copy(
            oi.at[kind, 3 + d], oi.at[kind, slot], h_s.at[kind, index], h_r.at[kind, index],
            jnp.where(near, other, remote), jnp.where(near, j, flip))

    def halo_in(kind, index):
        slot = jnp.where(core == 0, jnp.where(index < 3, 2 - index, 16 - index), jnp.where(index < 3, 11 + index, index - 3))
        return remote_copy(oi.at[kind, slot], oi.at[kind, slot], h_s.at[kind, index], h_r.at[kind, index], other, j)

    def has_halo(u):
        q = unit(u)[1]
        return (q < 3) | (q >= 5)

    def own_seen(d):
        return pltpu.make_async_copy(seen.at[d], oi.at[0, 3 + d, j], w_s.at[d])

    for k in FAR_FIRST:
        spread_nodes(k, 0).start()
    for copy in small:
        copy.wait()
    slot8 = lax.broadcasted_iota(jnp.int32, (256, 8), 0)
    cols[...] = jnp.where(slot8 < count[...], node[...].T, -1)
    xy = pos[:, pl.ds(pl.multiple_of(j * 256, 256), 256)].astype(jnp.float32).T
    for d in range(8):
        for axis in range(2):
            spot[axis, d] = jnp.broadcast_to(xy[:, 8 * axis + d:8 * axis + d + 1], (256, 128))
        total[d] = jnp.zeros((256, 1024), jnp.float32)

    def observe(q):
        d, n = district(q), turn(q)
        load(n).wait()
        lane = lax.broadcasted_iota(jnp.int32, (256, 8), 1)
        which = jnp.sum(jnp.where(lane == d, cols[...], 0), axis=1, keepdims=True)
        hot = jnp.where(lax.broadcasted_iota(jnp.int32, (256, 2048), 1) == which, 1.0, 0.0).astype(jnp.bfloat16)
        rows = jnp.dot(hot, held[lax.rem(n, 2)], preferred_element_type=jnp.float32)
        seen[d] = rows.astype(jnp.bfloat16)
        spots = lax.dot_general(pos[...], hot, (((1,), (1,)), ((), ())), preferred_element_type=jnp.float32)
        row16 = lax.broadcasted_iota(jnp.int32, (16, 256), 0)
        row8 = lax.broadcasted_iota(jnp.int32, (8, 256), 0)
        sx = jnp.sum(jnp.where(row16 == d, spots, 0.0), axis=0, keepdims=True)
        sy = jnp.sum(jnp.where(row16 == d + 8, spots, 0.0), axis=0, keepdims=True)
        sv = jnp.sum(jnp.where(row8 == d, var[...].astype(jnp.float32), 0.0), axis=0, keepdims=True)
        meta[3 + d] = jnp.where(row8 == 0, sx, jnp.where(row8 == 1, sy, jnp.where(row8 == 2, sv, 0.0)))

        @pl.when(n < 6)
        def _():
            load(n + 2).start()

        own_seen(d).start()

    far_meta = remote_copy(
        meta.at[pl.ds(3 + 5 * core, 3)], meta.at[pl.ds(11 - 11 * core, 3)], m_s.at[0], m_r.at[0], remote, flip)
    near_meta = remote_copy(
        meta.at[pl.ds(8 - 5 * core, 3)], meta.at[pl.ds(11 * core, 3)], m_s.at[1], m_r.at[1], other, j)

    def slot_of(qe):
        return 3 + qe + core * (7 - 2 * qe)

    def bring(kind, slot, which):
        @pl.when(kind == 0)
        def _():
            pltpu.make_async_copy(oi.at[0, slot], obs.at[slot], v_s.at[which]).start()

        @pl.when(kind == 1)
        def _():
            pltpu.make_async_copy(oi.at[1, slot], inn.at[slot], v_s.at[which]).start()

    def brought(kind, slot, which):
        @pl.when(kind == 0)
        def _():
            pltpu.make_async_copy(oi.at[0, slot], obs.at[slot], v_s.at[which]).wait()
            square = jnp.zeros((256, 128), jnp.float32)
            for m in range(8):
                part = obs[slot, m].astype(jnp.float32)
                square = square + part * part
            square = jnp.sum(square.T, axis=0, keepdims=True)
            inv[pl.ds(slot, 1)] = 1.0 / (square + 1023.0 * meta[slot, 2:3])

        @pl.when(kind == 1)
        def _():
            pltpu.make_async_copy(oi.at[1, slot], inn.at[slot], v_s.at[which]).wait()

    def own_event(t, act):
        u = t - 3 * LAG

        @pl.when((u >= 0) & (u < UNITS))
        def _():
            kind, q, d, s, three = unit(u)
            act(kind, 3 + d, 0)

    def near_event(t, act, first):
        u = t - 3 * LAG - 1

        @pl.when((u >= 6) & (u < 12))
        def _():
            kind, q, d, s, three = unit(u)
            if first:
                halo_in(kind, q - 2).wait_recv()
            act(kind, slot_of(15 - q), 1)

    def far_event(t, act, first):
        early = t < 16
        i = jnp.where(early, t - 10, t - 17) // 2

        @pl.when((t == 10) | (t == 12) | (t == 14) | (t == 17) | (t == 19) | (t == 21))
        def _():
            kind = jnp.where(early, 0, 1)
            if first:
                halo_in(kind, i).wait_recv()
            act(kind, slot_of(-1 - i), 2)

    def nodes_event(t):
        for q in range(8):
            @pl.when(t == X_STEP[q])
            def _():
                d = district(q)
                if q == 0:
                    own_x.wait()
                for k in range(1, 8):
                    source = mem_of(lax.rem(zl + k // 4, 2), y + 4 - k % 4)
                    block = xo.at[d, source]
                    remote_copy(block, block, a_s.at[k - 1, q], a_r.at[k - 1, q], di, flip).wait_recv()
                pltpu.make_async_copy(xo.at[d], xs.at[d], x_s).start()

            @pl.when(t == X_STEP[q] + 1)
            def _():
                pltpu.make_async_copy(xo.at[district(q)], xs.at[district(q)], x_s).wait()

    def tasks(t, table, first):
        code = jnp.int32(0)
        for i, word in enumerate(table):
            if word:
                code = jnp.where(t == first + i, word, code)
        return code

    def places(code, i):
        item = lax.rem(code // (128 ** i), 128)
        d, slot = district(lax.rem(item, 8)), slot_of(item // 8 - 3)
        return d, slot, slot - d

    def joined(ref, index):
        return jnp.concatenate([ref[index, m] for m in range(8)], axis=1)

    def gain_block(t):
        code = tasks(t, GAIN_TABLE, GAIN_FIRST)

        @pl.when((t >= GAIN_FIRST) & (t < GAIN_FIRST + len(GAIN_TABLE)))
        def _():
            for i in range(4):
                d, slot, s = places(code, i)
                cov = lax.dot_general(joined(xs, d), joined(obs, slot), (((1,), (1,)), ((), ())), preferred_element_type=jnp.float32)
                row = inv[pl.ds(slot, 1)] * flags[d, s].astype(jnp.float32)
                node_x, node_y = spot[0, d], spot[1, d]
                weight = taper(
                    jnp.concatenate([node_x, node_x], axis=1), jnp.concatenate([node_y, node_y], axis=1),
                    meta[slot], (s - RADIUS).astype(jnp.float32))
                gains[d, s] = (weight * cov * row).astype(jnp.bfloat16)

    def increment_block(t):
        code = tasks(t, INC_TABLE, INC_FIRST)

        @pl.when(code > 0)
        def _():
            for i in range(4):
                d, slot, s = places(code, i)
                total[d] += jnp.dot(gains[d, s], joined(inn, slot), preferred_element_type=jnp.float32)

    def finish(q):
        d = district(q)
        return pltpu.make_async_copy(total.at[d], out.at[d], o_s.at[q])

    def step(t, carry):
        @pl.when(t < UNITS)
        def _():
            kind, q, d, s, three = unit(t)
            targets = (mem_of(zl, y + s), mem_of(zl, y - s), flip)

            @pl.when(kind == 0)
            def _():
                observe(q)
                for edge in range(3):
                    edge_copy(t, edge, seen.at[d], oi.at[0, 3 + d, j], targets[edge]).start()

            @pl.when(kind == 1)
            def _():
                for edge in range(3):
                    edge_copy(t, edge, innov.at[d], oi.at[1, 3 + d, j], targets[edge]).start()

        @pl.when((t >= 1) & (t < 11) & (lax.rem(t, 3) < 2))
        def _():
            for k in FAR_FIRST:
                spread_nodes(k, t - t // 3).start()

        @pl.when(t == 3)
        def _():
            far_meta.start()

        @pl.when(t == 9)
        def _():
            far_meta.wait_recv()

        @pl.when(t == 11)
        def _():
            near_meta.start()

        @pl.when(t == 13)
        def _():
            near_meta.wait_recv()

        own_event(t - 1, brought)
        near_event(t - 1, brought, False)
        far_event(t - 1, brought, False)

        u = t - LAG

        @pl.when((u >= 0) & (u < UNITS))
        def _():
            for edge in range(3):
                gathered(u, edge).wait_recv()
                forward(u, edge + 3).start()

        v = t - 2 * LAG

        @pl.when((v >= 0) & (v < UNITS))
        def _():
            gathered_last(v, True)
            forward(v, 6).start()

        w = t - 3 * LAG

        @pl.when((w >= 0) & (w < UNITS))
        def _():
            gathered_last(w, False)
            gathered(w, 5).wait_recv()
            gathered(w, 6).wait_recv()
            kind, q, d, s, three = unit(w)

            @pl.when(kind == 0)
            def _():
                own_seen(d).wait()

            @pl.when(w == 3)
            def _():
                own_innov.wait()

            @pl.when(has_halo(w))
            def _():
                halo(w).start()

        own_event(t, bring)
        near_event(t, bring, True)
        far_event(t, bring, True)
        nodes_event(t)
        gain_block(t)
        increment_block(t)

        @pl.when(t == STEPS - 2)
        def _():
            for q in (0, 1, 2, 7):
                finish(q).start()

        return carry

    def gathered_last(u, first):
        three = unit(u)[4]
        take4 = three if first else jnp.logical_not(three)

        @pl.when(take4)
        def _():
            gathered(u, 4).wait_recv()

        @pl.when(jnp.logical_not(take4))
        def _():
            gathered(u, 3).wait_recv()

    lax.fori_loop(0, STEPS, step, 0)
    for q in (3, 4, 5, 6):
        finish(q).start()

    def drain(u, carry):
        for edge in range(7):
            gathered(u, edge).wait_send()

        @pl.when(has_halo(u))
        def _():
            halo(u).wait_send()

        return carry

    lax.fori_loop(0, UNITS, drain, 0)

    def drain_nodes(q, carry):
        for k in range(1, 8):
            spread_nodes(k, q).wait_send()
        return carry

    lax.fori_loop(0, 8, drain_nodes, 0)
    far_meta.wait_send()
    near_meta.wait_send()
    for q in range(8):
        finish(q).wait()


def taper(node_x, node_y, meta, shift):
    dx = (meta[0:1] + shift) - node_x
    dy = meta[1:2] - node_y
    square = jnp.maximum((dx * dx + dy * dy) * (1.0 / (REACH * REACH)), 1e-30)
    root = lax.rsqrt(square)
    z = square * root
    inner = (((-0.25 * z + 0.5) * z + 0.625) * z - 5.0 / 3.0) * square + 1.0
    left = jnp.maximum(2.0 - z, 0.0)
    left = left * left
    outer = (left * left) * (z * (1.0 / 12.0) + (1.0 / 6.0) - root * (1.0 / 24.0))
    return jnp.where(z < 1.0, inner, outer)


def analysis(anomalies, innovations, obs_var, node_pos, obs_node, obs_count, in_radius):
    bf16, f32 = jnp.bfloat16, jnp.float32
    return pl.pallas_call(
        analysis_kernel,
        out_shape=(
            jax.ShapeDtypeStruct((8, 256, 1024), f32),
            jax.ShapeDtypeStruct((8, 8, 256, 128), bf16),
            jax.ShapeDtypeStruct((2, 14, 8, 256, 128), bf16),
        ),
        in_specs=[HBM] * 6 + [SMEM],
        out_specs=(HBM,) * 3,
        scratch_shapes=[
            pltpu.VMEM((2, 2048, 128), bf16),
            pltpu.VMEM((8, 256, 128), bf16),
            pltpu.VMEM((14, 8, 256), f32),
            pltpu.VMEM((8, 256), jnp.int32),
            pltpu.VMEM((1, 8), jnp.int32),
            pltpu.VMEM((16, 2048), bf16),
            pltpu.VMEM((8, 256), bf16),
            pltpu.VMEM((256, 8), jnp.int32),
            pltpu.VMEM((8, 8, 256, 128), bf16),
            pltpu.VMEM((14, 8, 256, 128), bf16),
            pltpu.VMEM((14, 8, 256, 128), bf16),
            pltpu.VMEM((8, 7, 256, 256), bf16),
            pltpu.VMEM((8, 256, 1024), f32),
            pltpu.VMEM((14, 256), f32),
            pltpu.VMEM((2, 8, 256, 128), f32),
            DMA((7, 8)), DMA((7, 8)), DMA((7, UNITS)), DMA((7, UNITS)), DMA((2, 6)), DMA((2, 6)), DMA((2,)), DMA((2,)),
            DMA((6,)), DMA((2,)), DMA((8,)), DMA((3,)), DMA, DMA((8,)),
        ],
        compiler_params=pltpu.CompilerParams(collective_id=0, has_side_effects=True, vmem_limit_bytes=58 << 20),
    )(anomalies, innovations, obs_node, obs_count.reshape(1, 8), node_pos.reshape(16, 2048), obs_var, in_radius)[0]


def on_device(*arrays):
    return analysis(*arrays)


def solution(mesh):
    return jax.shard_map(
        on_device,
        mesh=mesh,
        in_specs=(
            P("dist", None, "mem"),
            P("dist", None, "mem"),
            P("dist", None),
            P(None, "dist", None),
            P("dist", None),
            P("dist"),
            P("dist", None),
        ),
        out_specs=P("dist", "mem", None),
        check_vma=False,
    )
```

time: 149 us -> 143 us (0.960)
  Pallas kernels: 147 us -> 134 us
  local copies, waits for them, and re-layouts: 0 us -> 8.44 us
    pallas_call x2 -> x1, Pallas kernels: 147 us -> 134 us  [analysis(): pl.pallas_call(analysis_kernel, out_shape=(jax.ShapeDtypeStruct((8, 256,...]
    unnamed x0 -> x1, local copies, waits for them, and re-layouts: none -> 8.44 us
where the time goes in v2:
time: 143 us; the launch traced here: 142 us
  Pallas kernels  134 us (94%)
  local copies, waits for them, and re-layouts  8.44 us (6%)
    pallas_call x1, Pallas kernels, analysis(): pl.pallas_call(analysis_kernel, out_shape=(jax.ShapeDtypeStruct((8, 256,...  134 us
    unnamed x1, local copies, waits for them, and re-layouts  8.44 us

profile of v2, /device:TPU:1, one launch (start us, length us, event | category | flops | bytes accessed | tf_op | source)
XLA Modules:
  0.0 142.4 jit_solution(8185793006025993063)
XLA Ops:
  0.0 134.0 %shard_map.73 = (f32[8,256,1024]{2,1,0:T(8,128)}, bf16[8,8,256,128]{3,2,1,0:T(8,128)(2,1)}, bf16[2,14,8,256,128]{4,3,2,1,0:T(8,128)(2,1)}) custom-call(bf16[8,2048,128]{2,1,0:T(8,128)(2,1)} %anom.1, bf16[8,256,128]{2,1,0:T(8,128)(2,1)} %innov.1, s32[8,256]{1,0:T(8,128)} %node_h.1, s32[1,8]{1,0:T(1,128)} %bitcast.3, bf16[16,2048]{1,0:T(8,128)(2,1)} %bitcast.2, ...), custom_call_target="tpu_custom_call" | custom-call | tf_op jit(solution)/shard_map/pallas_call | solution.py:482
  134.0 8.4 %copy.9 = f32[8,256,1024]{2,1,0:T(8,128)} copy(f32[8,256,1024]{2,1,0:T(8,128)} %get-tuple-element.6) | data formatting | bytes 16777216

commit v3 on v2

--- a/solution.py
+++ b/solution.py
@@ -15,56 +15,64 @@
 UNITS = 16
 LAG = 2
 FAR_FIRST = (6, 2, 5, 7, 4, 1, 3)
-STEPS = 25
-X_STEP = (4, 5, 7, 8, 10, 11, 13, 14)
-
-
-def column(*parts):
-    items = [(e + 3) * 8 + d for e, own in parts for d in own]
-    return sum(item * 128 ** i for i, item in enumerate(items))
-
-
-GAIN_FIRST = 9
+STEPS = 22
+OWN_USED = 14
+NODE_TURN = (1, 0, 2, 3, 4, 5, 6, 7)
+
+
+def column(*pairs):
+    return sum(((e + 3) * 8 + d) * 128 ** i for i, (e, d) in enumerate(pairs))
+
+
+GAIN_FIRST = 8
 GAIN_TABLE = (
-    column((0, (0, 1, 2, 3))),
-    column((1, (0, 1, 2, 3))),
-    column((1, (4,)), (-1, (0, 1, 2))),
-    column((2, (0, 1, 2, 3))),
-    column((2, (4, 5)), (-2, (0, 1))),
-    column((7, (4, 5, 6)), (8, (5,))),
-    column((7, (7,)), (8, (6, 7)), (-3, (0,))),
-    column((6, (3, 4, 5, 6))),
-    column((6, (7,)), (9, (6, 7)), (5, (2,))),
-    column((5, (3, 4, 5, 6))),
-    column((5, (7,)), (10, (7,)), (4, (1, 2))),
-    column((4, (3, 4, 5, 6))),
-    column((4, (7,)), (3, (0, 1, 2))),
-    column((3, (3, 4, 5, 6))),
+    column((0, 0), (0, 1), (1, 0), (1, 1)),
+    column((0, 2), (1, 2), (2, 0), (2, 1)),
+    column((2, 2), (3, 0), (3, 1), (3, 2)),
+    column((0, 3), (1, 3), (-1, 0), (-1, 1)),
+    column((-1, 2), (2, 3), (4, 1), (4, 2)),
+    column((1, 4), (2, 4), (-2, 0), (-2, 1)),
+    column((5, 2), (5, 3), (5, 4), (4, 3)),
+    column((2, 5), (6, 3), (6, 4), (6, 5)),
+    column((-3, 0), (5, 5), (4, 4), (4, 5)),
+    column((7, 4), (7, 5), (7, 6), (6, 6)),
+    column((8, 5), (8, 6), (5, 6), (9, 6)),
+    column((7, 7), (6, 7), (8, 7), (5, 7)),
+    column((9, 7), (4, 6), (4, 7), (10, 7)),
+    column((3, 3), (3, 4), (3, 5), (3, 6)),
 )
-INC_FIRST = 10
+INC_FIRST = 12
 INC_TABLE = (
-    column((0, (0, 1, 2, 3))),
-    column((1, (0, 1, 2, 3))),
-    column((1, (4,)), (2, (0, 1, 2))),
+    column((0, 0), (0, 1), (0, 2), (0, 3)),
     0,
-    column((2, (3, 4, 5)), (7, (4,))),
-    column((7, (5, 6, 7)), (8, (5,))),
-    column((8, (6, 7)), (6, (3, 4))),
-    column((6, (5, 6, 7)), (9, (6,))),
-    column((9, (7,)), (-1, (0, 1, 2))),
-    column((5, (2, 3, 4, 5))),
-    column((5, (6, 7)), (10, (7,)), (-2, (0,))),
-    column((-2, (1,)), (4, (1, 2, 3))),
-    column((4, (4, 5, 6, 7))),
-    column((-3, (0,)), (3, (0, 1, 2))),
-    column((3, (3, 4, 5, 6))),
+    column((1, 0), (1, 1), (1, 2), (1, 3)),
+    0,
+    column((1, 4), (2, 0), (2, 1), (2, 2)),
+    column((-1, 0), (-1, 1), (-1, 2), (2, 3)),
+    column((2, 4), (2, 5), (-2, 0), (-2, 1)),
+    column((7, 4), (7, 5), (7, 6), (7, 7)),
+    column((6, 3), (6, 4), (6, 5), (6, 6)),
+    column((8, 5), (8, 6), (6, 7), (8, 7)),
 )
+LATE = (
+    (-3, 3,),
+    (3, 4,),
+    (3, 4, 5,),
+    (3, 4, 5,),
+    (3, 4, 5,),
+    (3, 4, 5,),
+    (3, 4, 5, 9,),
+    (4, 5, 9, 10,),
+)
+
+
+MOST = max(len(others) for others in LATE)
 
 
 def analysis_kernel(
-    anom, innov, node_h, count_h, pos_h, var_h, flags, out, xo, oi,
+    anom, innov, node_h, count_h, pos_h, var_h, flags, out, late, xo, oi,
     held, seen, meta, node, count, pos, var, cols, xs, obs, inn, gains, total, inv, spot,
-    a_s, a_r, g_s, g_r, h_s, h_r, m_s, m_r, l_s, p_s, w_s, v_s, x_s, o_s,
+    a_s, a_r, g_s, g_r, h_s, h_r, m_s, m_r, l_s, p_s, w_s, v_s, x_s, o_s, f_s,
 ):
     di, j = lax.axis_index("dist"), lax.axis_index("mem")
     core = lax.rem(di, 2)
@@ -85,11 +93,8 @@
     for copy in small:
         copy.start()
 
-    def turn(n):
-        return jnp.where(n < 3, n, 10 - n)
-
     def load(n):
-        return pltpu.make_async_copy(anom.at[district(turn(n))], held.at[lax.rem(n, 2)], p_s.at[lax.rem(n, 2)])
+        return pltpu.make_async_copy(anom.at[district(n)], held.at[lax.rem(n, 2)], p_s.at[lax.rem(n, 2)])
 
     load(0).start()
     load(1).start()
@@ -106,6 +111,8 @@
         pl.semaphore_signal(barrier, inc=1, device_id={"dist": di, "mem": lax.rem(j + k, 8)}, device_id_type=MESH)
     pl.semaphore_signal(barrier, inc=1, device_id={"dist": other, "mem": j}, device_id_type=MESH)
     pl.semaphore_signal(barrier, inc=1, device_id={"dist": remote, "mem": flip}, device_id_type=MESH)
+    for d in range(8):
+        total[d] = jnp.zeros((256, 1024), jnp.float32)
     pl.semaphore_wait(barrier, 9)
 
     def remote_copy(source, target, send, recv, dist, mem):
@@ -121,9 +128,10 @@
             a_s.at[k - 1, q], a_r.at[k - 1, q], di, target)
 
     def unit(u):
-        early = u < 6
-        kind = jnp.where(early, u // 3, lax.rem(u, 2))
-        q = jnp.where(early, lax.rem(u, 3), 10 - u // 2)
+        middle = (u >= 5) & (u < 11)
+        odd = lax.rem(u, 2)
+        kind = jnp.where(middle, odd, jnp.where(u < 5, 0, 1))
+        q = jnp.where(middle, jnp.where(odd == 1, (u - 5) // 2, 2 + u // 2), jnp.where(u < 5, u, 18 - u))
         return kind, q, district(q), 1 - 2 * lax.rem(u, 2), lax.rem(u, 3) == 2
 
     def edge_copy(u, edge, source, block, mem):
@@ -177,8 +185,8 @@
     def own_seen(d):
         return pltpu.make_async_copy(seen.at[d], oi.at[0, 3 + d, j], w_s.at[d])
 
-    for k in FAR_FIRST:
-        spread_nodes(k, 0).start()
+    for k in FAR_FIRST[:3]:
+        spread_nodes(k, NODE_TURN[0]).start()
     for copy in small:
         copy.wait()
     slot8 = lax.broadcasted_iota(jnp.int32, (256, 8), 0)
@@ -187,10 +195,9 @@
     for d in range(8):
         for axis in range(2):
             spot[axis, d] = jnp.broadcast_to(xy[:, 8 * axis + d:8 * axis + d + 1], (256, 128))
-        total[d] = jnp.zeros((256, 1024), jnp.float32)
 
     def observe(q):
-        d, n = district(q), turn(q)
+        d, n = district(q), q
         load(n).wait()
         lane = lax.broadcasted_iota(jnp.int32, (256, 8), 1)
         which = jnp.sum(jnp.where(lane == d, cols[...], 0), axis=1, keepdims=True)
@@ -246,7 +253,7 @@
     def own_event(t, act):
         u = t - 3 * LAG
 
-        @pl.when((u >= 0) & (u < UNITS))
+        @pl.when((u >= 0) & (u < OWN_USED))
         def _():
             kind, q, d, s, three = unit(u)
             act(kind, 3 + d, 0)
@@ -254,7 +261,7 @@
     def near_event(t, act, first):
         u = t - 3 * LAG - 1
 
-        @pl.when((u >= 6) & (u < 12))
+        @pl.when((u == 6) | (u == 8) | ((u >= 10) & (u < 14)))
         def _():
             kind, q, d, s, three = unit(u)
             if first:
@@ -262,32 +269,39 @@
             act(kind, slot_of(15 - q), 1)
 
     def far_event(t, act, first):
-        early = t < 16
-        i = jnp.where(early, t - 10, t - 17) // 2
-
-        @pl.when((t == 10) | (t == 12) | (t == 14) | (t == 17) | (t == 19) | (t == 21))
+        early = t < 15
+        i = jnp.where(early, t - 10, t - 15) // 2
+
+        @pl.when((t == 10) | (t == 12) | (t == 14) | (t == 15) | (t == 17) | (t == 19))
         def _():
             kind = jnp.where(early, 0, 1)
             if first:
                 halo_in(kind, i).wait_recv()
             act(kind, slot_of(-1 - i), 2)
 
+    def nodes_copy(q):
+        return pltpu.make_async_copy(xo.at[district(q)], xs.at[district(q)], x_s)
+
     def nodes_event(t):
-        for q in range(8):
-            @pl.when(t == X_STEP[q])
-            def _():
-                d = district(q)
-                if q == 0:
-                    own_x.wait()
-                for k in range(1, 8):
-                    source = mem_of(lax.rem(zl + k // 4, 2), y + 4 - k % 4)
-                    block = xo.at[d, source]
-                    remote_copy(block, block, a_s.at[k - 1, q], a_r.at[k - 1, q], di, flip).wait_recv()
-                pltpu.make_async_copy(xo.at[d], xs.at[d], x_s).start()
-
-            @pl.when(t == X_STEP[q] + 1)
-            def _():
-                pltpu.make_async_copy(xo.at[district(q)], xs.at[district(q)], x_s).wait()
+        turn = t // 2 - 2
+        q = jnp.where(turn < 2, 1 - turn, turn)
+
+        @pl.when(t == 4)
+        def _():
+            own_x.wait()
+
+        @pl.when((turn >= 0) & (turn < 8) & (lax.rem(t, 2) == 0))
+        def _():
+            d = district(q)
+            for k in range(1, 8):
+                source = mem_of(lax.rem(zl + k // 4, 2), y + 4 - k % 4)
+                block = xo.at[d, source]
+                remote_copy(block, block, a_s.at[k - 1, q], a_r.at[k - 1, q], di, flip).wait_recv()
+            nodes_copy(q).start()
+
+        @pl.when((turn >= 0) & (turn < 8) & (lax.rem(t, 2) == 1))
+        def _():
+            nodes_copy(q).wait()
 
     def tasks(t, table, first):
         code = jnp.int32(0)
@@ -304,12 +318,12 @@
     def joined(ref, index):
         return jnp.concatenate([ref[index, m] for m in range(8)], axis=1)
 
-    def gain_block(t):
+    def gain_block(t, part):
         code = tasks(t, GAIN_TABLE, GAIN_FIRST)
 
         @pl.when((t >= GAIN_FIRST) & (t < GAIN_FIRST + len(GAIN_TABLE)))
         def _():
-            for i in range(4):
+            for i in part:
                 d, slot, s = places(code, i)
                 cov = lax.dot_general(joined(xs, d), joined(obs, slot), (((1,), (1,)), ((), ())), preferred_element_type=jnp.float32)
                 row = inv[pl.ds(slot, 1)] * flags[d, s].astype(jnp.float32)
@@ -328,6 +342,14 @@
                 d, slot, s = places(code, i)
                 total[d] += jnp.dot(gains[d, s], joined(inn, slot), preferred_element_type=jnp.float32)
 
+    def hand_over():
+        copies = []
+        for q, others in enumerate(LATE):
+            for r, e in enumerate(others):
+                d = district(q)
+                copies.append(pltpu.make_async_copy(gains.at[d, slot_of(e) - d], late.at[d, r], f_s.at[q, r]))
+        return copies
+
     def finish(q):
         d = district(q)
         return pltpu.make_async_copy(total.at[d], out.at[d], o_s.at[q])
@@ -349,10 +371,18 @@
                 for edge in range(3):
                     edge_copy(t, edge, innov.at[d], oi.at[1, 3 + d, j], targets[edge]).start()
 
-        @pl.when((t >= 1) & (t < 11) & (lax.rem(t, 3) < 2))
-        def _():
-            for k in FAR_FIRST:
-                spread_nodes(k, t - t // 3).start()
+        turn = t // 2
+        place = jnp.where(turn < 2, 1 - turn, turn)
+
+        @pl.when((t >= 1) & (t < 16) & (lax.rem(t, 2) == 0))
+        def _():
+            for k in FAR_FIRST[:3]:
+                spread_nodes(k, place).start()
+
+        @pl.when((t < 16) & (lax.rem(t, 2) == 1))
+        def _():
+            for k in FAR_FIRST[3:]:
+                spread_nodes(k, place).start()
 
         @pl.when(t == 3)
         def _():
@@ -382,12 +412,25 @@
                 gathered(u, edge).wait_recv()
                 forward(u, edge + 3).start()
 
+        nodes_event(t)
+        gain_block(t, (0, 1))
+
         v = t - 2 * LAG
 
         @pl.when((v >= 0) & (v < UNITS))
         def _():
             gathered_last(v, True)
             forward(v, 6).start()
+
+        gain_block(t, (2, 3))
+        increment_block(t)
+
+        @pl.when(t == STEPS - 1)
+        def _():
+            for copy in hand_over():
+                copy.start()
+            for q in range(8):
+                finish(q).start()
 
         w = t - 3 * LAG
 
@@ -413,15 +456,6 @@
         own_event(t, bring)
         near_event(t, bring, True)
         far_event(t, bring, True)
-        nodes_event(t)
-        gain_block(t)
-        increment_block(t)
-
-        @pl.when(t == STEPS - 2)
-        def _():
-            for q in (0, 1, 2, 7):
-                finish(q).start()
-
         return carry
 
     def gathered_last(u, first):
@@ -437,8 +471,7 @@
             gathered(u, 3).wait_recv()
 
     lax.fori_loop(0, STEPS, step, 0)
-    for q in (3, 4, 5, 6):
-        finish(q).start()
+    near_event(jnp.int32(STEPS - 1), brought, False)
 
     def drain(u, carry):
         for edge in range(7):
@@ -462,6 +495,8 @@
     near_meta.wait_send()
     for q in range(8):
         finish(q).wait()
+    for copy in hand_over():
+        copy.wait()
 
 
 def taper(node_x, node_y, meta, shift):
@@ -483,11 +518,12 @@
         analysis_kernel,
         out_shape=(
             jax.ShapeDtypeStruct((8, 256, 1024), f32),
+            jax.ShapeDtypeStruct((8, MOST, 256, 256), bf16),
             jax.ShapeDtypeStruct((8, 8, 256, 128), bf16),
             jax.ShapeDtypeStruct((2, 14, 8, 256, 128), bf16),
         ),
         in_specs=[HBM] * 6 + [SMEM],
-        out_specs=(HBM,) * 3,
+        out_specs=(HBM,) * 4,
         scratch_shapes=[
             pltpu.VMEM((2, 2048, 128), bf16),
             pltpu.VMEM((8, 256, 128), bf16),
@@ -505,14 +541,80 @@
             pltpu.VMEM((14, 256), f32),
             pltpu.VMEM((2, 8, 256, 128), f32),
             DMA((7, 8)), DMA((7, 8)), DMA((7, UNITS)), DMA((7, UNITS)), DMA((2, 6)), DMA((2, 6)), DMA((2,)), DMA((2,)),
-            DMA((6,)), DMA((2,)), DMA((8,)), DMA((3,)), DMA, DMA((8,)),
+            DMA((6,)), DMA((2,)), DMA((8,)), DMA((3,)), DMA, DMA((8,)), DMA((8, MOST)),
         ],
         compiler_params=pltpu.CompilerParams(collective_id=0, has_side_effects=True, vmem_limit_bytes=58 << 20),
-    )(anomalies, innovations, obs_node, obs_count.reshape(1, 8), node_pos.reshape(16, 2048), obs_var, in_radius)[0]
+    )(anomalies, innovations, obs_node, obs_count.reshape(1, 8), node_pos.reshape(16, 2048), obs_var, in_radius)
+
+
+def closing_kernel(flags, total, late_h, oi, out, gains, inn, i_s, g_s):
+    d = pl.program_id(0)
+    core = lax.rem(lax.axis_index("dist"), 2)
+
+    def slot_of(qe):
+        return 3 + qe + core * (7 - 2 * qe)
+
+    used = sorted({e for others in LATE for e in others})
+    innovations = [
+        pltpu.make_async_copy(oi.at[1, slot_of(e)], inn.at[slot_of(e)], i_s.at[i]) for i, e in enumerate(used)]
+    gains_in = pltpu.make_async_copy(late_h, gains, g_s)
+
+    @pl.when(d == 0)
+    def _():
+        gains_in.start()
+        for copy in innovations:
+            copy.start()
+
+    out[0] = total[0]
+
+    @pl.when(d == 0)
+    def _():
+        gains_in.wait()
+        for copy in innovations:
+            copy.wait()
+
+    q = d + core * (7 - 2 * d)
+    code = jnp.int32(0)
+    for place, others in enumerate(LATE):
+        code = jnp.where(q == place, sum((e + 4) * 16 ** r for r, e in enumerate(others)), code)
+
+    def add(r, code):
+        item = lax.rem(code, 16)
+        slot = slot_of(item - 4)
+        s = jnp.clip(slot - d, 0, 6)
+
+        @pl.when((item > 0) & (flags[d, s] > 0))
+        def _():
+            rows = jnp.concatenate([inn[slot, m] for m in range(8)], axis=1)
+            out[0] += jnp.dot(gains[d, r], rows, preferred_element_type=jnp.float32)
+
+        return code // 16
+
+    lax.fori_loop(0, MOST, add, code)
+
+
+def closing(in_radius, total, late, oi):
+    used = len({e for others in LATE for e in others})
+    block = pl.BlockSpec((1, 256, 1024), lambda d: (d, 0, 0))
+    return pl.pallas_call(
+        closing_kernel,
+        grid=(8,),
+        out_shape=jax.ShapeDtypeStruct((8, 256, 1024), jnp.float32),
+        in_specs=[SMEM, block, HBM, HBM],
+        out_specs=block,
+        scratch_shapes=[
+            pltpu.VMEM((8, MOST, 256, 256), jnp.bfloat16),
+            pltpu.VMEM((14, 8, 256, 128), jnp.bfloat16),
+            DMA((used,)),
+            DMA,
+        ],
+        compiler_params=pltpu.CompilerParams(vmem_limit_bytes=56 << 20),
+    )(in_radius, total, late, oi)
 
 
 def on_device(*arrays):
-    return analysis(*arrays)
+    total, late, xo, oi = analysis(*arrays)
+    return closing(arrays[-1], total, late, oi)
 
 
 def solution(mesh):

time: 143 us -> 143 us (level)
  the two profiles are of different devices: /device:TPU:1 before, /device:TPU:32 now
where the time goes in v3:
time: 143 us; the launch traced here: 142 us
  Pallas kernels  142 us (99%)
    pallas_call x1, Pallas kernels, analysis(): pl.pallas_call(analysis_kernel, out_shape=(jax.ShapeDtypeStruct((8, 256,...  127 us
    pallas_call x1, Pallas kernels, closing(): pl.pallas_call(closing_kernel, grid=(8,), out_shape=jax.ShapeDtypeStruct(...  15.2 us

profile of v3, /device:TPU:32, one launch (start us, length us, event | category | flops | bytes accessed | tf_op | source)
XLA Modules:
  0.0 141.7 jit_solution(17160437091171907952)
XLA Ops:
  0.0 126.5 %shard_map.73 = (f32[8,256,1024]{2,1,0:T(8,128)}, bf16[8,4,256,256]{3,2,1,0:T(8,128)(2,1)}, bf16[8,8,256,128]{3,2,1,0:T(8,128)(2,1)}, bf16[2,14,8,256,128]{4,3,2,1,0:T(8,128)(2,1)}) custom-call(bf16[8,2048,128]{2,1,0:T(8,128)(2,1)} %anom.1, bf16[8,256,128]{2,1,0:T(8,128)(2,1)} %innov.1, s32[8,256]{1,0:T(8,128)} %node_h.1, s32[1,8]{1,0:T(1,128)} %bitcast.3, ...), custom_call_target="tpu_custom_call" | custom-call | tf_op jit(solution)/shard_map/pallas_call | solution.py:517
  126.5 15.2 %shard_map.74 = f32[8,256,1024]{2,1,0:T(8,128)} custom-call(s32[8,7]{1,0:T(8,128)} %flags.3, f32[8,256,1024]{2,1,0:T(8,128)} %get-tuple-element.8.total, bf16[8,4,256,256]{3,2,1,0:T(8,128)(2,1)} %get-tuple-element.9.late_h, bf16[2,14,8,256,128]{4,3,2,1,0:T(8,128)(2,1)} %get-tuple-element.10.oi), custom_call_target="tpu_custom_call" | custom-call | tf_op jit(solution)/shard_map/pallas_call | solution.py:599

commit v4 on v3

--- a/solution.py
+++ b/solution.py
@@ -52,7 +52,6 @@
     column((2, 4), (2, 5), (-2, 0), (-2, 1)),
     column((7, 4), (7, 5), (7, 6), (7, 7)),
     column((6, 3), (6, 4), (6, 5), (6, 6)),
-    column((8, 5), (8, 6), (6, 7), (8, 7)),
 )
 LATE = (
     (-3, 3,),
@@ -60,12 +59,13 @@
     (3, 4, 5,),
     (3, 4, 5,),
     (3, 4, 5,),
-    (3, 4, 5,),
-    (3, 4, 5, 9,),
-    (4, 5, 9, 10,),
+    (3, 4, 5, 8,),
+    (3, 4, 5, 8, 9,),
+    (4, 5, 6, 8, 9, 10,),
 )
 
 
+LAST_GAINS = ((3, 3), (3, 4), (3, 5), (3, 6))
 MOST = max(len(others) for others in LATE)
 
 
@@ -282,15 +282,18 @@
     def nodes_copy(q):
         return pltpu.make_async_copy(xo.at[district(q)], xs.at[district(q)], x_s)
 
-    def nodes_event(t):
+    def nodes_turn(t):
         turn = t // 2 - 2
-        q = jnp.where(turn < 2, 1 - turn, turn)
+        return (turn >= 0) & (turn < 8), jnp.where(turn < 2, 1 - turn, turn)
+
+    def nodes_arrive(t):
+        due, q = nodes_turn(t)
 
         @pl.when(t == 4)
         def _():
             own_x.wait()
 
-        @pl.when((turn >= 0) & (turn < 8) & (lax.rem(t, 2) == 0))
+        @pl.when(due & (lax.rem(t, 2) == 0))
         def _():
             d = district(q)
             for k in range(1, 8):
@@ -299,7 +302,10 @@
                 remote_copy(block, block, a_s.at[k - 1, q], a_r.at[k - 1, q], di, flip).wait_recv()
             nodes_copy(q).start()
 
-        @pl.when((turn >= 0) & (turn < 8) & (lax.rem(t, 2) == 1))
+    def nodes_ready(t):
+        due, q = nodes_turn(t)
+
+        @pl.when(due & (lax.rem(t, 2) == 1))
         def _():
             nodes_copy(q).wait()
 
@@ -342,10 +348,12 @@
                 d, slot, s = places(code, i)
                 total[d] += jnp.dot(gains[d, s], joined(inn, slot), preferred_element_type=jnp.float32)
 
-    def hand_over():
+    def hand_over(last):
         copies = []
         for q, others in enumerate(LATE):
             for r, e in enumerate(others):
+                if ((e, q) in LAST_GAINS) != last:
+                    continue
                 d = district(q)
                 copies.append(pltpu.make_async_copy(gains.at[d, slot_of(e) - d], late.at[d, r], f_s.at[q, r]))
         return copies
@@ -400,9 +408,11 @@
         def _():
             near_meta.wait_recv()
 
+
         own_event(t - 1, brought)
         near_event(t - 1, brought, False)
         far_event(t - 1, brought, False)
+        nodes_ready(t)
 
         u = t - LAG
 
@@ -412,9 +422,6 @@
                 gathered(u, edge).wait_recv()
                 forward(u, edge + 3).start()
 
-        nodes_event(t)
-        gain_block(t, (0, 1))
-
         v = t - 2 * LAG
 
         @pl.when((v >= 0) & (v < UNITS))
@@ -422,12 +429,9 @@
             gathered_last(v, True)
             forward(v, 6).start()
 
-        gain_block(t, (2, 3))
-        increment_block(t)
-
         @pl.when(t == STEPS - 1)
         def _():
-            for copy in hand_over():
+            for copy in hand_over(False):
                 copy.start()
             for q in range(8):
                 finish(q).start()
@@ -456,6 +460,9 @@
         own_event(t, bring)
         near_event(t, bring, True)
         far_event(t, bring, True)
+        nodes_arrive(t)
+        gain_block(t, (0, 1, 2, 3))
+        increment_block(t)
         return carry
 
     def gathered_last(u, first):
@@ -471,7 +478,8 @@
             gathered(u, 3).wait_recv()
 
     lax.fori_loop(0, STEPS, step, 0)
-    near_event(jnp.int32(STEPS - 1), brought, False)
+    for copy in hand_over(True):
+        copy.start()
 
     def drain(u, carry):
         for edge in range(7):
@@ -495,7 +503,7 @@
     near_meta.wait_send()
     for q in range(8):
         finish(q).wait()
-    for copy in hand_over():
+    for copy in hand_over(False) + hand_over(True):
         copy.wait()
 
 
@@ -547,7 +555,7 @@
     )(anomalies, innovations, obs_node, obs_count.reshape(1, 8), node_pos.reshape(16, 2048), obs_var, in_radius)
 
 
-def closing_kernel(flags, total, late_h, oi, out, gains, inn, i_s, g_s):
+def closing_kernel(flags, total_h, late_h, oi, out, total, gains, inn, i_s, g_s, t_s):
     d = pl.program_id(0)
     core = lax.rem(lax.axis_index("dist"), 2)
 
@@ -557,19 +565,32 @@
     used = sorted({e for others in LATE for e in others})
     innovations = [
         pltpu.make_async_copy(oi.at[1, slot_of(e)], inn.at[slot_of(e)], i_s.at[i]) for i, e in enumerate(used)]
-    gains_in = pltpu.make_async_copy(late_h, gains, g_s)
+
+    def sums(i):
+        return pltpu.make_async_copy(total_h.at[i], total.at[i], t_s.at[i])
+
+    def weights(i, r):
+        return pltpu.make_async_copy(late_h.at[i, r], gains.at[i, r], g_s.at[i, r])
 
     @pl.when(d == 0)
     def _():
-        gains_in.start()
-        for copy in innovations:
-            copy.start()
-
-    out[0] = total[0]
+        for i in range(8):
+            sums(i).start()
+            for r in range(MOST):
+                counts = [len(others) > r for others in LATE]
+
+                @pl.when(jnp.where(core == 0, int(counts[i]), int(counts[7 - i])) > 0)
+                def _():
+                    weights(i, r).start()
+            if i == 0:
+                for copy in innovations:
+                    copy.start()
+
+    sums(d).wait()
+    out[0] = total[d]
 
     @pl.when(d == 0)
     def _():
-        gains_in.wait()
         for copy in innovations:
             copy.wait()
 
@@ -582,6 +603,10 @@
         item = lax.rem(code, 16)
         slot = slot_of(item - 4)
         s = jnp.clip(slot - d, 0, 6)
+
+        @pl.when(item > 0)
+        def _():
+            weights(d, r).wait()
 
         @pl.when((item > 0) & (flags[d, s] > 0))
         def _():
@@ -600,13 +625,15 @@
         closing_kernel,
         grid=(8,),
         out_shape=jax.ShapeDtypeStruct((8, 256, 1024), jnp.float32),
-        in_specs=[SMEM, block, HBM, HBM],
+        in_specs=[SMEM, HBM, HBM, HBM],
         out_specs=block,
         scratch_shapes=[
+            pltpu.VMEM((8, 256, 1024), jnp.float32),
             pltpu.VMEM((8, MOST, 256, 256), jnp.bfloat16),
             pltpu.VMEM((14, 8, 256, 128), jnp.bfloat16),
             DMA((used,)),
-            DMA,
+            DMA((8, MOST)),
+            DMA((8,)),
         ],
         compiler_params=pltpu.CompilerParams(vmem_limit_bytes=56 << 20),
     )(in_radius, total, late, oi)

time: 143 us -> 138 us (0.965)
  the two profiles are of different devices: /device:TPU:32 before, /device:TPU:1 now
where the time goes in v4:
time: 138 us
  Pallas kernels  138 us (100%)
    pallas_call x1, Pallas kernels, analysis(): pl.pallas_call(analysis_kernel, out_shape=(jax.ShapeDtypeStruct((8, 256,...  123 us
    pallas_call x1, Pallas kernels, closing(): pl.pallas_call(closing_kernel, grid=(8,), out_shape=jax.ShapeDtypeStruct(...  14.8 us

profile of v4, /device:TPU:1, one launch (start us, length us, event | category | flops | bytes accessed | tf_op | source)
XLA Modules:
  0.0 137.6 jit_solution(9377800372116901781)
XLA Ops:
  0.0 122.8 %shard_map.73 = (f32[8,256,1024]{2,1,0:T(8,128)}, bf16[8,6,256,256]{3,2,1,0:T(8,128)(2,1)}, bf16[8,8,256,128]{3,2,1,0:T(8,128)(2,1)}, bf16[2,14,8,256,128]{4,3,2,1,0:T(8,128)(2,1)}) custom-call(bf16[8,2048,128]{2,1,0:T(8,128)(2,1)} %anom.1, bf16[8,256,128]{2,1,0:T(8,128)(2,1)} %innov.1, s32[8,256]{1,0:T(8,128)} %node_h.1, s32[1,8]{1,0:T(1,128)} %bitcast.3, ...), custom_call_target="tpu_custom_call" | custom-call | tf_op jit(solution)/shard_map/pallas_call | solution.py:525
  122.8 14.8 %shard_map.74 = f32[8,256,1024]{2,1,0:T(8,128)} custom-call(s32[8,7]{1,0:T(8,128)} %flags.3, f32[8,256,1024]{2,1,0:T(8,128)} %get-tuple-element.8.total_h, bf16[8,6,256,256]{3,2,1,0:T(8,128)(2,1)} %get-tuple-element.9.late_h, bf16[2,14,8,256,128]{4,3,2,1,0:T(8,128)(2,1)} %get-tuple-element.10.oi), custom_call_target="tpu_custom_call" | custom-call | tf_op jit(solution)/shard_map/pallas_call | solution.py:624

commit v5 on v4

--- a/solution.py
+++ b/solution.py
@@ -98,10 +98,12 @@
 
     load(0).start()
     load(1).start()
-    own_x = pltpu.make_async_copy(anom.at[:, pl.ds(pl.multiple_of(j * 256, 256), 256), :], xo.at[:, j], l_s.at[4])
-    own_innov = pltpu.make_async_copy(innov, oi.at[1, pl.ds(3, 8), j], l_s.at[5])
-    own_x.start()
-    own_innov.start()
+    take_x = pltpu.make_async_copy(anom.at[:, pl.ds(pl.multiple_of(j * 256, 256), 256), :], xs.at[:, j], l_s.at[4])
+    take_innov = pltpu.make_async_copy(innov, inn.at[pl.ds(3, 8), j], l_s.at[5])
+    own_x = pltpu.make_async_copy(xs.at[:, j], xo.at[:, j], l_s.at[4])
+    own_innov = pltpu.make_async_copy(inn.at[pl.ds(3, 8), j], oi.at[1, pl.ds(3, 8), j], l_s.at[5])
+    take_x.start()
+    take_innov.start()
 
     flip = mem_of(1 - zl, y)
     other = di + 1 - 2 * core
@@ -187,8 +189,10 @@
 
     for k in FAR_FIRST[:3]:
         spread_nodes(k, NODE_TURN[0]).start()
-    for copy in small:
+    for copy in small + [take_x, take_innov]:
         copy.wait()
+    own_x.start()
+    own_innov.start()
     slot8 = lax.broadcasted_iota(jnp.int32, (256, 8), 0)
     cols[...] = jnp.where(slot8 < count[...], node[...].T, -1)
     xy = pos[:, pl.ds(pl.multiple_of(j * 256, 256), 256)].astype(jnp.float32).T
@@ -379,19 +383,6 @@
                 for edge in range(3):
                     edge_copy(t, edge, innov.at[d], oi.at[1, 3 + d, j], targets[edge]).start()
 
-        turn = t // 2
-        place = jnp.where(turn < 2, 1 - turn, turn)
-
-        @pl.when((t >= 1) & (t < 16) & (lax.rem(t, 2) == 0))
-        def _():
-            for k in FAR_FIRST[:3]:
-                spread_nodes(k, place).start()
-
-        @pl.when((t < 16) & (lax.rem(t, 2) == 1))
-        def _():
-            for k in FAR_FIRST[3:]:
-                spread_nodes(k, place).start()
-
         @pl.when(t == 3)
         def _():
             far_meta.start()
@@ -435,6 +426,19 @@
                 copy.start()
             for q in range(8):
                 finish(q).start()
+
+        turn = t // 2
+        place = jnp.where(turn < 2, 1 - turn, turn)
+
+        @pl.when((t >= 1) & (t < 16) & (lax.rem(t, 2) == 0))
+        def _():
+            for k in FAR_FIRST[:3]:
+                spread_nodes(k, place).start()
+
+        @pl.when((t < 16) & (lax.rem(t, 2) == 1))
+        def _():
+            for k in FAR_FIRST[3:]:
+                spread_nodes(k, place).start()
 
         w = t - 3 * LAG
 
@@ -555,8 +559,7 @@
     )(anomalies, innovations, obs_node, obs_count.reshape(1, 8), node_pos.reshape(16, 2048), obs_var, in_radius)
 
 
-def closing_kernel(flags, total_h, late_h, oi, out, total, gains, inn, i_s, g_s, t_s):
-    d = pl.program_id(0)
+def closing_kernel(flags, total_h, late_h, oi, out, total, gains, inn, i_s, g_s, t_s, o_s):
     core = lax.rem(lax.axis_index("dist"), 2)
 
     def slot_of(qe):
@@ -566,73 +569,81 @@
     innovations = [
         pltpu.make_async_copy(oi.at[1, slot_of(e)], inn.at[slot_of(e)], i_s.at[i]) for i, e in enumerate(used)]
 
-    def sums(i):
-        return pltpu.make_async_copy(total_h.at[i], total.at[i], t_s.at[i])
-
-    def weights(i, r):
-        return pltpu.make_async_copy(late_h.at[i, r], gains.at[i, r], g_s.at[i, r])
-
-    @pl.when(d == 0)
-    def _():
-        for i in range(8):
-            sums(i).start()
-            for r in range(MOST):
-                counts = [len(others) > r for others in LATE]
-
-                @pl.when(jnp.where(core == 0, int(counts[i]), int(counts[7 - i])) > 0)
-                def _():
-                    weights(i, r).start()
-            if i == 0:
-                for copy in innovations:
-                    copy.start()
-
-    sums(d).wait()
-    out[0] = total[d]
-
-    @pl.when(d == 0)
-    def _():
-        for copy in innovations:
-            copy.wait()
-
-    q = d + core * (7 - 2 * d)
-    code = jnp.int32(0)
-    for place, others in enumerate(LATE):
-        code = jnp.where(q == place, sum((e + 4) * 16 ** r for r, e in enumerate(others)), code)
-
-    def add(r, code):
-        item = lax.rem(code, 16)
-        slot = slot_of(item - 4)
-        s = jnp.clip(slot - d, 0, 6)
-
-        @pl.when(item > 0)
-        def _():
-            weights(d, r).wait()
-
-        @pl.when((item > 0) & (flags[d, s] > 0))
-        def _():
-            rows = jnp.concatenate([inn[slot, m] for m in range(8)], axis=1)
-            out[0] += jnp.dot(gains[d, r], rows, preferred_element_type=jnp.float32)
-
-        return code // 16
-
-    lax.fori_loop(0, MOST, add, code)
+    def sums(d):
+        return pltpu.make_async_copy(total_h.at[d], total.at[d], t_s.at[d])
+
+    def result(d):
+        return pltpu.make_async_copy(total.at[d], out.at[d], o_s.at[d])
+
+    def weights(d, r):
+        return pltpu.make_async_copy(late_h.at[d, r], gains.at[d, r], g_s.at[d, r])
+
+    def each(d, act):
+        q = d + core * (7 - 2 * d)
+        code = jnp.int32(0)
+        for place, others in enumerate(LATE):
+            code = jnp.where(q == place, sum((e + 4) * 16 ** r for r, e in enumerate(others)), code)
+
+        def one(r, code):
+            item = lax.rem(code, 16)
+            slot = jnp.clip(slot_of(item - 4), 0, 13)
+            s = jnp.clip(slot - d, 0, 6)
+
+            @pl.when((item > 0) & (flags[d, s] > 0))
+            def _():
+                act(d, r, slot)
+
+            return code // 16
+
+        lax.fori_loop(0, MOST, one, code)
+
+    sums(0).start()
+    for copy in innovations:
+        copy.start()
+
+    def fetch(d, carry):
+        each(d, lambda d, r, slot: weights(d, r).start())
+
+        @pl.when(d > 0)
+        def _():
+            sums(d).start()
+
+        return carry
+
+    lax.fori_loop(0, 8, fetch, 0)
+    for copy in innovations:
+        copy.wait()
+
+    def add(d, r, slot):
+        weights(d, r).wait()
+        rows = jnp.concatenate([inn[slot, m] for m in range(8)], axis=1)
+        total[d] += jnp.dot(gains[d, r], rows, preferred_element_type=jnp.float32)
+
+    def close(d, carry):
+        sums(d).wait()
+        each(d, add)
+        result(d).start()
+        return carry
+
+    lax.fori_loop(0, 8, close, 0)
+    for d in range(8):
+        result(d).wait()
 
 
 def closing(in_radius, total, late, oi):
     used = len({e for others in LATE for e in others})
-    block = pl.BlockSpec((1, 256, 1024), lambda d: (d, 0, 0))
     return pl.pallas_call(
         closing_kernel,
-        grid=(8,),
         out_shape=jax.ShapeDtypeStruct((8, 256, 1024), jnp.float32),
         in_specs=[SMEM, HBM, HBM, HBM],
-        out_specs=block,
+        out_specs=HBM,
         scratch_shapes=[
             pltpu.VMEM((8, 256, 1024), jnp.float32),
             pltpu.VMEM((8, MOST, 256, 256), jnp.bfloat16),
             pltpu.VMEM((14, 8, 256, 128), jnp.bfloat16),
             DMA((used,)),
             DMA((8, MOST)),
+            DMA((8,)),
             DMA((8,)),
         ],
         compiler_params=pltpu.CompilerParams(vmem_limit_bytes=56 << 20),

time: 138 us -> 133 us (0.964); the launches traced: 138 us -> 131 us
  Pallas kernels: 138 us -> 131 us
    pallas_call x1, Pallas kernels: 14.8 us -> 8.71 us  [closing(): pl.pallas_call(closing_kernel, out_shape=jax.ShapeDtypeStruct((8, 256, 10...]
where the time goes in v5:
time: 133 us; the launch traced here: 131 us
  Pallas kernels  131 us (98%)
    pallas_call x1, Pallas kernels, analysis(): pl.pallas_call(analysis_kernel, out_shape=(jax.ShapeDtypeStruct((8, 256,...  122 us
    pallas_call x1, Pallas kernels, closing(): pl.pallas_call(closing_kernel, out_shape=jax.ShapeDtypeStruct((8, 256, 10...  8.71 us

profile of v5, /device:TPU:1, one launch (start us, length us, event | category | flops | bytes accessed | tf_op | source)
XLA Modules:
  0.0 130.8 jit_solution(16885468132802933272)
XLA Ops:
  0.0 122.1 %shard_map.73 = (f32[8,256,1024]{2,1,0:T(8,128)}, bf16[8,6,256,256]{3,2,1,0:T(8,128)(2,1)}, bf16[8,8,256,128]{3,2,1,0:T(8,128)(2,1)}, bf16[2,14,8,256,128]{4,3,2,1,0:T(8,128)(2,1)}) custom-call(bf16[8,2048,128]{2,1,0:T(8,128)(2,1)} %anom.1, bf16[8,256,128]{2,1,0:T(8,128)(2,1)} %innov.1, s32[8,256]{1,0:T(8,128)} %node_h.1, s32[1,8]{1,0:T(1,128)} %bitcast.3, ...), custom_call_target="tpu_custom_call" | custom-call | tf_op jit(solution)/shard_map/pallas_call | solution.py:529
  122.1 8.7 %shard_map.74 = f32[8,256,1024]{2,1,0:T(8,128)} custom-call(s32[8,7]{1,0:T(8,128)} %flags.3, f32[8,256,1024]{2,1,0:T(8,128)} %get-tuple-element.8.total_h, bf16[8,6,256,256]{3,2,1,0:T(8,128)(2,1)} %get-tuple-element.9.late_h, bf16[2,14,8,256,128]{4,3,2,1,0:T(8,128)(2,1)} %get-tuple-element.10.oi), custom_call_target="tpu_custom_call" | custom-call | tf_op jit(solution)/shard_map/pallas_call | solution.py:635

commit v6 on v5

--- a/solution.py
+++ b/solution.py
@@ -566,8 +566,20 @@
         return 3 + qe + core * (7 - 2 * qe)
 
     used = sorted({e for others in LATE for e in others})
-    innovations = [
-        pltpu.make_async_copy(oi.at[1, slot_of(e)], inn.at[slot_of(e)], i_s.at[i]) for i, e in enumerate(used)]
+    first = [min(place for place, others in enumerate(LATE) if e in others) for e in used]
+
+    def district(q):
+        return q + core * (7 - 2 * q)
+
+    wanted = [
+        sum(flags[district(place), slot_of(e) - district(place)] for place, others in enumerate(LATE) if e in others)
+        for e in used]
+
+    def innovations(q, act):
+        for i, e in enumerate(used):
+            @pl.when((q == first[i]) & (wanted[i] > 0))
+            def _():
+                act(pltpu.make_async_copy(oi.at[1, slot_of(e)], inn.at[slot_of(e)], i_s.at[i]))
 
     def sums(d):
         return pltpu.make_async_copy(total_h.at[d], total.at[d], t_s.at[d])
@@ -578,8 +590,8 @@
     def weights(d, r):
         return pltpu.make_async_copy(late_h.at[d, r], gains.at[d, r], g_s.at[d, r])
 
-    def each(d, act):
-        q = d + core * (7 - 2 * d)
+    def each(q, act):
+        d = district(q)
         code = jnp.int32(0)
         for place, others in enumerate(LATE):
             code = jnp.where(q == place, sum((e + 4) * 16 ** r for r, e in enumerate(others)), code)
@@ -597,32 +609,24 @@
 
         lax.fori_loop(0, MOST, one, code)
 
-    sums(0).start()
-    for copy in innovations:
-        copy.start()
-
-    def fetch(d, carry):
-        each(d, lambda d, r, slot: weights(d, r).start())
-
-        @pl.when(d > 0)
-        def _():
-            sums(d).start()
-
+    def fetch(q, carry):
+        sums(district(q)).start()
+        innovations(q, lambda copy: copy.start())
+        each(q, lambda d, r, slot: weights(d, r).start())
         return carry
 
     lax.fori_loop(0, 8, fetch, 0)
-    for copy in innovations:
-        copy.wait()
 
     def add(d, r, slot):
         weights(d, r).wait()
         rows = jnp.concatenate([inn[slot, m] for m in range(8)], axis=1)
         total[d] += jnp.dot(gains[d, r], rows, preferred_element_type=jnp.float32)
 
-    def close(d, carry):
-        sums(d).wait()
-        each(d, add)
-        result(d).start()
+    def close(q, carry):
+        sums(district(q)).wait()
+        innovations(q, lambda copy: copy.wait())
+        each(q, add)
+        result(district(q)).start()
         return carry
 
     lax.fori_loop(0, 8, close, 0)

time: 133 us -> 133 us (level); the launches traced: 131 us -> 133 us
  Pallas kernels: 131 us -> 133 us
    pallas_call x1, Pallas kernels: 8.71 us -> 10.7 us  [closing(): pl.pallas_call(closing_kernel, out_shape=jax.ShapeDtypeStruct((8, 256, 10...]
where the time goes in v6:
time: 133 us
  Pallas kernels  133 us (100%)
    pallas_call x1, Pallas kernels, analysis(): pl.pallas_call(analysis_kernel, out_shape=(jax.ShapeDtypeStruct((8, 256,...  122 us
    pallas_call x1, Pallas kernels, closing(): pl.pallas_call(closing_kernel, out_shape=jax.ShapeDtypeStruct((8, 256, 10...  10.7 us

profile of v6, /device:TPU:1, one launch (start us, length us, event | category | flops | bytes accessed | tf_op | source)
XLA Modules:
  0.0 132.8 jit_solution(1488913601554153615)
XLA Ops:
  0.0 122.1 %shard_map.73 = (f32[8,256,1024]{2,1,0:T(8,128)}, bf16[8,6,256,256]{3,2,1,0:T(8,128)(2,1)}, bf16[8,8,256,128]{3,2,1,0:T(8,128)(2,1)}, bf16[2,14,8,256,128]{4,3,2,1,0:T(8,128)(2,1)}) custom-call(bf16[8,2048,128]{2,1,0:T(8,128)(2,1)} %anom.1, bf16[8,256,128]{2,1,0:T(8,128)(2,1)} %innov.1, s32[8,256]{1,0:T(8,128)} %node_h.1, s32[1,8]{1,0:T(1,128)} %bitcast.3, ...), custom_call_target="tpu_custom_call" | custom-call | tf_op jit(solution)/shard_map/pallas_call | solution.py:529
  122.1 10.7 %shard_map.74 = f32[8,256,1024]{2,1,0:T(8,128)} custom-call(s32[8,7]{1,0:T(8,128)} %flags.3, f32[8,256,1024]{2,1,0:T(8,128)} %get-tuple-element.8.total_h, bf16[8,6,256,256]{3,2,1,0:T(8,128)(2,1)} %get-tuple-element.9.late_h, bf16[2,14,8,256,128]{4,3,2,1,0:T(8,128)(2,1)} %get-tuple-element.10.oi), custom_call_target="tpu_custom_call" | custom-call | tf_op jit(solution)/shard_map/pallas_call | solution.py:639

commit v7 on v5

--- a/solution.py
+++ b/solution.py
@@ -375,12 +375,12 @@
             @pl.when(kind == 0)
             def _():
                 observe(q)
-                for edge in range(3):
+                for edge in (2, 0, 1):
                     edge_copy(t, edge, seen.at[d], oi.at[0, 3 + d, j], targets[edge]).start()
 
             @pl.when(kind == 1)
             def _():
-                for edge in range(3):
+                for edge in (2, 0, 1):
                     edge_copy(t, edge, innov.at[d], oi.at[1, 3 + d, j], targets[edge]).start()
 
         @pl.when(t == 3)

time: 133 us -> 132 us (level)
  no operation moved by 1% of the time
where the time goes in v7:
time: 132 us; the launch traced here: 131 us
  Pallas kernels  131 us (99%)
    pallas_call x1, Pallas kernels, analysis(): pl.pallas_call(analysis_kernel, out_shape=(jax.ShapeDtypeStruct((8, 256,...  122 us
    pallas_call x1, Pallas kernels, closing(): pl.pallas_call(closing_kernel, out_shape=jax.ShapeDtypeStruct((8, 256, 10...  8.74 us

profile of v7, /device:TPU:1, one launch (start us, length us, event | category | flops | bytes accessed | tf_op | source)
XLA Modules:
  0.0 130.8 jit_solution(15979440830874551931)
XLA Ops:
  0.0 122.1 %shard_map.73 = (f32[8,256,1024]{2,1,0:T(8,128)}, bf16[8,6,256,256]{3,2,1,0:T(8,128)(2,1)}, bf16[8,8,256,128]{3,2,1,0:T(8,128)(2,1)}, bf16[2,14,8,256,128]{4,3,2,1,0:T(8,128)(2,1)}) custom-call(bf16[8,2048,128]{2,1,0:T(8,128)(2,1)} %anom.1, bf16[8,256,128]{2,1,0:T(8,128)(2,1)} %innov.1, s32[8,256]{1,0:T(8,128)} %node_h.1, s32[1,8]{1,0:T(1,128)} %bitcast.3, ...), custom_call_target="tpu_custom_call" | custom-call | tf_op jit(solution)/shard_map/pallas_call | solution.py:529
  122.1 8.7 %shard_map.74 = f32[8,256,1024]{2,1,0:T(8,128)} custom-call(s32[8,7]{1,0:T(8,128)} %flags.3, f32[8,256,1024]{2,1,0:T(8,128)} %get-tuple-element.8.total_h, bf16[8,6,256,256]{3,2,1,0:T(8,128)(2,1)} %get-tuple-element.9.late_h, bf16[2,14,8,256,128]{4,3,2,1,0:T(8,128)(2,1)} %get-tuple-element.10.oi), custom_call_target="tpu_custom_call" | custom-call | tf_op jit(solution)/shard_map/pallas_call | solution.py:635
